TPU v7x, 32 devices: a whole 2x2x4 slice. The times are simulated.
32 devices in a mesh: groups: 2 (over y), track: 4 (over z), expert: 4 (over x, core).
Axes of the slice: x: 2, y: 2, z: 4, core: 2. Of those that a mesh axis runs over, the one named last changes fastest.
Arguments:
- states: bfloat16 [4, 2048, 2048], P('track', ('groups', 'expert')), parts along dimension 1, may hold values from -3 to 3
- routes: int32 [4, 2048, 2], P('track', ('groups', 'expert')), parts along dimension 1, may hold values from 0 to 3, all different within a row; in each aligned block of 256 rows (0 to 255, 256 to 511, ..., all dimensions but the last counted through in order) at most 256 rows name the same one
- route_gates: float32 [4, 2048, 2], P('track', ('groups', 'expert')), parts along dimension 1, may hold values from 0.2 to 1
- norm_gain: float32 [4, 2048], P('track'), may hold values from 0.1 to 1.9
- w_gate: bfloat16 [4, 4, 2048, 768], P('track', 'expert'), may hold values from -0.125 to 0.125
- w_up: bfloat16 [4, 4, 2048, 768], P('track', 'expert'), may hold values from -0.125 to 0.125
- w_down: bfloat16 [4, 4, 768, 2048], P('track', 'expert'), may hold values from -0.21875 to 0.21875
Outputs:
- mixed: bfloat16 [2048, 2048], P(('groups', 'expert'), 'track'), parts along dimension 0
There are 2 independent parts, one for each index of `groups`. A program takes and returns all parts, laid end to end along the dimension named above; an argument that names none is the same for every part. Nothing has to cross between parts.
Inputs may be any that keep to these rules, and one draw needn't show every extreme that they name: `routes`: each token names 2 different experts of its track. Within each track, among the 256 tokens of one index of expert (aligned blocks of the token dimension), no expert is named by more than 256 tokens, and in every draw some expert is named by exactly 256 tokens of some block.
All inputs are finite; a program needn't handle non-finite values.
Results may differ from a plain program's by a relative error of at most 0.023.
Values may be sent and summed in bfloat16 or wider, within the bound.
No kernel may reach another device: no remote copies, remote signals or barrier semaphores. Data moves between devices by JAX's collectives and lax.ppermute only.
A program may use at most 64 MiB of HBM per device.

v0:
```python
import functools

import jax
import jax.numpy as jnp
from jax import lax
from jax.experimental import pallas as pl
from jax.experimental.pallas import tpu as pltpu
from jax.sharding import PartitionSpec as P

CHUNKS = (1, 1, 1, 1)
HOP, START, WIRE, EXPERT = 1.5, 2.2, 22.5, 12.0
ROWS_FIRST = 2


def slot_places(chosen, experts, capacity):
    flat_ids = chosen.reshape(-1)
    labels = jnp.arange(experts, dtype=jnp.int32)
    matches = (flat_ids[:, None] == labels[None, :]).astype(jnp.int32)
    earlier = jnp.cumsum(matches, axis=0) - matches
    slot_index = jnp.sum(earlier * matches, axis=1)
    return flat_ids * capacity + slot_index


def expert_hidden(arrived, gate_w, up_w, exp_dev):
    sources = arrived.shape[0] // exp_dev
    grouped = arrived.reshape(sources, exp_dev, arrived.shape[1], arrived.shape[2])
    gate_part = jnp.einsum("secd,edf->secf", grouped, gate_w, preferred_element_type=jnp.float32)
    up_part = jnp.einsum("secd,edf->secf", grouped, up_w, preferred_element_type=jnp.float32)
    return (jax.nn.silu(gate_part) * up_part).astype(jnp.bfloat16)


def dispatched(states, routes, route_gates, norm_gain, w_gate, w_up, w_down):
    summed_entry = lax.psum(states[0], "track").astype(jnp.float32)
    tok_rows, model_width = summed_entry.shape
    top_count = routes.shape[2]
    exp_dev = w_gate.shape[1]
    experts = exp_dev * lax.axis_size("expert")
    tracks = lax.axis_size("track")
    capacity = 4 * tok_rows // experts
    slice_width = model_width // tracks
    inverse_rms = lax.rsqrt(jnp.mean(summed_entry * summed_entry, axis=1, keepdims=True) + 1e-06)
    normed = (summed_entry * inverse_rms * norm_gain[0][None, :]).astype(jnp.bfloat16)
    places = slot_places(routes[0], experts, capacity)
    row_owner = jnp.full((experts * capacity,), tok_rows, jnp.int32)
    row_owner = row_owner.at[places].set(
        jnp.arange(top_count * tok_rows, dtype=jnp.int32) // top_count
    )
    outbound = jnp.take(normed, row_owner, axis=0, mode="fill", fill_value=0).reshape(
        experts, capacity, model_width
    )
    own_slice = lax.dynamic_slice_in_dim(
        summed_entry, lax.axis_index("track") * slice_width, slice_width, 1
    )
    arrived = lax.all_to_all(outbound, "expert", split_axis=0, concat_axis=0, tiled=True)
    count_items = arrived.shape[1]
    hidden = expert_hidden(arrived, w_gate[0], w_up[0], exp_dev)
    result = jnp.einsum(
        "secf,efd->secd", hidden, w_down[0], preferred_element_type=jnp.float32
    ).astype(jnp.bfloat16)
    returned = lax.all_to_all(
        result.reshape(experts, count_items, model_width),
        "expert",
        split_axis=0,
        concat_axis=0,
        tiled=True,
    )
    picked = jnp.take(returned.reshape(-1, model_width), places, axis=0)
    branch = jnp.sum(
        picked.reshape(tok_rows, top_count, model_width) * route_gates[0][:, :, None], axis=1
    )
    summed = lax.psum_scatter(
        branch.astype(jnp.bfloat16), "track", scatter_dimension=1, tiled=True
    ).astype(jnp.float32)
    return (own_slice + summed).astype(jnp.bfloat16)


def swap(value, axis, bit):
    size = lax.axis_size(axis)
    return lax.ppermute(value, axis, [(i, i ^ bit) for i in range(size)])


def bits_of(size):
    out, bit = [], 1
    while bit < size:
        out.append(bit)
        bit *= 2
    return out


VMEM = pl.BlockSpec(memory_space=pltpu.VMEM)
ANY = pl.BlockSpec(memory_space=pl.ANY)


def call(body, outs, ins, extra=(), scratch=(), limit=4, space=VMEM):
    count = len(ins)

    def kernel(*refs):
        body(*refs[:count], *refs[count + len(extra) :])

    return pl.pallas_call(
        kernel,
        out_shape=outs,
        in_specs=[space] * len(ins) + [ANY] * len(extra),
        out_specs=[VMEM] * len(outs),
        scratch_shapes=scratch,
        compiler_params=pltpu.CompilerParams(vmem_limit_bytes=limit * 1024 * 1024),
    )(*ins, *extra)


def half_of(*shape):
    return jax.ShapeDtypeStruct(shape, jnp.bfloat16)


def full_of(*shape):
    return jax.ShapeDtypeStruct(shape, jnp.float32)


def add_body(*refs):
    total = refs[0][...].astype(jnp.float32)
    for ref in refs[1:-1]:
        total = total + ref[...].astype(jnp.float32)
    refs[-1][...] = total.astype(jnp.bfloat16)


def pick_body(step, mine, came, out):
    tracks, me = lax.axis_size("track"), lax.axis_index("track")
    takes = (me == step) | (me == tracks - 1 - step)
    out[...] = jnp.where(takes, came[...], mine[...])


def tile_of(size, want):
    while size % want:
        want //= 2
    return want


def table_body(routes, gates, out):
    for expert in range(out.shape[0]):
        named = jnp.where(routes[...] == expert, gates[...], 0.0)
        out[expert : expert + 1] = jnp.sum(named, axis=0, keepdims=True)


def turn_body(near, *refs):
    out = refs[-1]
    me = lax.axis_index("expert")
    for place, ref in enumerate(refs[:-1]):
        table = ref[...]
        rows = table.shape[1]
        labels = lax.broadcasted_iota(jnp.int32, table.shape, 0)
        picked = [
            jnp.sum(jnp.where(labels == named, table, 0.0), axis=0, keepdims=True)
            for named in (me, me ^ near)
        ]
        wide = jnp.concatenate(picked + [jnp.zeros((6, rows), jnp.float32)], axis=0)
        out[place] = jnp.transpose(wide)


def split_body(whole, *refs):
    parts, sems = refs[:-1], refs[-1]
    copies, start = [], 0
    for place, part in enumerate(parts):
        copies.append(
            pltpu.make_async_copy(whole.at[start : start + part.shape[0]], part, sems.at[place])
        )
        copies[-1].start()
        start += part.shape[0]
    for copy in copies:
        copy.wait()


def expert_body(piece, first, sources, gain, weight, gates, ups, downs, keep, send, normed, hidden):
    rows = sources[0].shape[0]
    ff = gates[0].shape[1]
    for place, ref in enumerate(sources):
        wide = ref[...].astype(jnp.float32)
        inverse = lax.rsqrt(jnp.mean(wide * wide, axis=1, keepdims=True) + 1e-06)
        normed[place * rows : (place + 1) * rows] = (wide * inverse * gain[...]).astype(jnp.bfloat16)
    block = tile_of(ff, 256)
    chosen = jnp.concatenate(
        [weight[place, first : first + rows] for place in range(len(sources))], axis=0
    )
    for expert, (gate, up) in enumerate(zip(gates, ups)):

        def hide(step, carry, expert=expert, gate=gate, up=up):
            at = pl.ds(pl.multiple_of(step * block, block), block)
            gate_part = jnp.dot(normed[...], gate[:, at], preferred_element_type=jnp.float32)
            up_part = jnp.dot(normed[...], up[:, at], preferred_element_type=jnp.float32)
            value = jax.nn.silu(gate_part) * up_part * chosen[:, expert : expert + 1]
            to = pl.ds(pl.multiple_of(expert * ff + step * block, block), block)
            hidden[:, to] = value.astype(jnp.bfloat16)
            return carry

        lax.fori_loop(0, ff // block, hide, 0, unroll=True)
    if keep.shape[1] == downs[0].shape[1]:
        half = keep.shape[0]

        def lower_all(step, carry):
            at = pl.ds(pl.multiple_of(step * piece, piece), piece)
            value = jnp.dot(hidden[:, :ff], downs[0][:, at], preferred_element_type=jnp.float32)
            for expert in range(1, len(downs)):
                value += jnp.dot(
                    hidden[:, expert * ff : (expert + 1) * ff],
                    downs[expert][:, at],
                    preferred_element_type=jnp.float32,
                )
            keep[:, at] = value[:half]
            send[:, at] = value[half:].astype(jnp.bfloat16)
            return carry

        lax.fori_loop(0, keep.shape[1] // piece, lower_all, 0, unroll=True)
        return
    parity = lax.axis_index("track") % 2
    for side, out in ((1 - parity, send), (parity, keep)):

        def lower(step, carry, side=side, out=out):
            at = pl.ds(pl.multiple_of((2 * step + side) * piece, piece), piece)
            value = jnp.dot(hidden[:, :ff], downs[0][:, at], preferred_element_type=jnp.float32)
            for expert in range(1, len(downs)):
                value += jnp.dot(
                    hidden[:, expert * ff : (expert + 1) * ff],
                    downs[expert][:, at],
                    preferred_element_type=jnp.float32,
                )
            to = pl.ds(pl.multiple_of(step * piece, piece), piece)
            out[:, to] = value.astype(out.dtype)
            return carry

        lax.fori_loop(0, out.shape[1] // piece, lower, 0, unroll=True)


def split_columns_body(bit, piece, kept, came, keep, send):
    parity = (lax.axis_index("track") // bit) % 2
    for step in range(keep.shape[1] // piece):
        to = slice(step * piece, (step + 1) * piece)
        for side, out in ((1 - parity, send), (parity, keep)):
            at = pl.ds(pl.multiple_of((2 * step + side) * piece, piece), piece)
            out[:, to] = (kept[:, at] + came[:, at].astype(jnp.float32)).astype(out.dtype)


def split_rows_body(kept, came, keep, send):
    rows = keep.shape[0]
    keep[...] = kept[:rows] + came[:rows].astype(jnp.float32)
    send[...] = (kept[rows:] + came[rows:].astype(jnp.float32)).astype(jnp.bfloat16)


def final_body(piece, starts, mine, kept, came, base, *refs):
    out = refs[-1]
    rows = kept.shape[0]
    at = pl.ds(pl.multiple_of(lax.axis_index("track") * piece, piece), piece)
    total = kept[...] + came[...].astype(jnp.float32) + base[:, at].astype(jnp.float32)
    out[starts[mine] : starts[mine] + rows] = total.astype(out.dtype)
    for place, ref in zip((c for c in range(len(starts)) if c != mine), refs[:-1]):
        out[starts[place] : starts[place] + ref.shape[0]] = ref[...]


def order_of(shares, plans, expert):
    free, ready, pending = {}, {}, {}
    now = 0.0

    def launch(c, at):
        link, amount = plans[c][at][1]
        begin = max(now, free.get(link, 0.0))
        free[link] = begin + amount * shares[c] * WIRE
        ready[c] = free[link] + HOP
        pending[c] = at

    def left(c):
        rest = plans[c][pending[c] :]
        return sum(amount * WIRE * shares[c] + HOP + START for _, (_, amount) in rest)

    for c in range(len(shares)):
        launch(c, 0)
    order = []
    while pending:
        now = max(now, min(ready[c] for c in pending))
        c = max((c for c in pending if ready[c] <= now), key=left)
        at = pending.pop(c)
        order.append((c, at))
        now += START + (EXPERT * shares[c] if plans[c][at][0] is expert else 0.1)
        if at + 1 < len(plans[c]):
            launch(c, at + 1)
    return order


def dense(states, routes, route_gates, norm_gain, w_gate, w_up, w_down):
    tok_rows, width = states.shape[1:]
    ff = w_gate.shape[3]
    experts, tracks = lax.axis_size("expert"), lax.axis_size("track")
    middle = tracks // 2
    piece = width // tracks
    far_bits = list(reversed(bits_of(experts)))[:-1]
    near = bits_of(experts)[0]
    groups = 2 ** len(far_bits)

    sizes = [tok_rows * part // sum(CHUNKS) for part in CHUNKS]
    starts = [sum(sizes[:c]) for c in range(len(sizes))]
    to_vmem = lambda value: pltpu.with_memory_space_constraint(value, pltpu.VMEM)

    weights = [
        (to_vmem(value[0, 0]), to_vmem(swap(value[0, 0], "expert", near)))
        for value in (w_gate, w_up, w_down)
    ]
    turned = [jnp.swapaxes(value, 1, 2)[0] for value in (routes, route_gates)]
    tables = list(call(table_body, [full_of(experts, tok_rows)], turned))
    for bit in far_bits:
        tables += [swap(value, "expert", bit) for value in tables]
    (chosen,) = call(
        functools.partial(turn_body, near), [full_of(groups, tok_rows, 8)], tables
    )
    last = [chosen]

    def run(body, outs, ins, **options):
        got = call(body, outs, ins, last[:1], **options)
        last[0] = got[-1]
        return got

    def trade(value, axis, bit):
        return lax.ppermute(value, axis, [(i, i ^ bit) for i in range(lax.axis_size(axis))])

    pieces = call(
        split_body,
        [half_of(size, width) for size in sizes],
        [states[0]],
        scratch=[pltpu.SemaphoreType.DMA((len(sizes),))],
        space=pl.BlockSpec(memory_space=pltpu.HBM),
    )

    inward = lambda s: [(s, s + 1), (tracks - 1 - s, tracks - 2 - s)]
    outward = lambda s: [(s, s - 1), (tracks - 1 - s, tracks - s)]
    across = [(middle - 1, middle), (middle, middle - 1)]

    state = [dict() for _ in sizes]
    result = [None]

    def begin(c):
        own = pieces[c]
        state[c]["sum"] = [own]
        state[c]["came"] = lax.ppermute(own, "track", inward(0) if middle > 1 else across)

    def gather(c, step):
        st = state[c]
        st["sum"].append(st["came"])
        (total,) = run(add_body, [half_of(sizes[c], width)], st["sum"])
        if step < middle - 1:
            link = inward(step + 1) if step + 1 < middle - 1 else across
            st["came"] = lax.ppermute(total, "track", link)
        else:
            st["total"] = total
            spread(c, middle - 1)

    def spread(c, step):
        st = state[c]
        if step > 0:
            st["came"] = lax.ppermute(st["total"], "track", outward(step))
        else:
            rows = st["total"]
            parts = [rows]
            for bit in far_bits:
                parts += [trade(value, "expert", bit) for value in parts]
            st["parts"] = parts

    def picked(c, step):
        st = state[c]
        (st["total"],) = run(
            functools.partial(pick_body, step - 1),
            [half_of(sizes[c], width)],
            [st["total"], st["came"]],
        )
        spread(c, step - 1)

    def expert(c):
        st = state[c]
        rows = sizes[c] * groups
        gates, ups, downs = weights

        def body(*refs):
            sources, refs = refs[:groups], refs[groups:]
            expert_body(
                piece, starts[c], sources, refs[0], refs[1], refs[2:4], refs[4:6], refs[6:8], *refs[8:]
            )

        rows_first = c >= len(sizes) - ROWS_FIRST
        shape = (rows // 2, width) if rows_first else (rows, width // 2)
        st["keep"], send = run(
            body,
            [full_of(*shape), half_of(*shape)],
            [*st["parts"], norm_gain, chosen, *gates, *ups, *downs],
            scratch=[pltpu.VMEM((rows, width), jnp.bfloat16), pltpu.VMEM((rows, 2 * ff), jnp.bfloat16)],
            limit=26,
        )
        if rows_first:
            st["came"] = trade(send, "expert", far_bits[-1])
        else:
            st["came"] = trade(send, "track", 1)

    def columns(c, bit):
        st = state[c]
        rows, count = st["keep"].shape
        st["keep"], send = run(
            functools.partial(split_columns_body, bit, piece),
            [full_of(rows, count // 2), half_of(rows, count // 2)],
            [st["keep"], st["came"]],
        )
        st["came"] = trade(send, "track", bit)

    def rows_of(c, bit):
        st = state[c]
        rows, count = st["keep"].shape
        st["keep"], send = run(
            split_rows_body,
            [full_of(rows // 2, count), half_of(rows // 2, count)],
            [st["keep"], st["came"]],
        )
        st["came"] = trade(send, "expert", bit)

    def final(c):
        st = state[c]
        ins = [st["keep"], st["came"], st["total"]]
        others = [other.get("out") for other in state if other is not st]
        if any(other is None for other in others):
            body = functools.partial(final_body, piece, (0,), 0)
            (st["out"],) = run(body, [half_of(sizes[c], piece)], ins)
        else:
            body = functools.partial(final_body, piece, starts, c)
            (result[0],) = run(body, [half_of(tok_rows, piece)], ins + others)

    steps = [(functools.partial(gather, step=step), ("in", 1.0)) for step in range(middle)]
    steps[-1] = (steps[-1][0], ("mid", 1.0))
    steps += [
        (functools.partial(picked, step=step), ("out", 1.0)) for step in range(middle - 1, 0, -1)
    ]
    steps += [(expert, ("x", 1.0))]

    def tail(rows_first):
        trades = [(rows_of, "x", bit) for bit in reversed(far_bits)]
        trades = [(columns, "z", bit) for bit in bits_of(tracks)] + trades
        if rows_first:
            trades = trades[len(bits_of(tracks)) :] + trades[: len(bits_of(tracks))]
        amount = 1.0 if groups > 1 else 0.5
        out = []
        for (_, link, bit), after in zip(trades, trades[1:] + [None]):
            if link == "z":
                link, load = ("out" if bit == 1 else "mid"), amount * bit
            else:
                load = amount
            amount /= 2
            if after is None:
                step = final
            else:
                step = functools.partial(after[0], bit=after[2])
            out.append((step, (link, load)))
        return out

    plans = []
    for c in range(len(sizes)):
        plans.append(steps + tail(c >= len(sizes) - ROWS_FIRST))
    shares = [size / tok_rows for size in sizes]
    for c in range(len(sizes)):
        begin(c)
    for c, at in order_of(shares, plans, expert):
        plans[c][at][0](c)
    return result[0]


def local(states, routes, route_gates, norm_gain, w_gate, w_up, w_down):
    tok_rows = states.shape[1]
    experts = w_gate.shape[1] * lax.axis_size("expert")
    if 4 * tok_rows // experts < tok_rows or w_gate.shape[1] != 1:
        return dispatched(states, routes, route_gates, norm_gain, w_gate, w_up, w_down)
    return dense(states, routes, route_gates, norm_gain, w_gate, w_up, w_down)


def solution(mesh):
    return jax.shard_map(
        local,
        mesh=mesh,
        in_specs=(
            P("track", ("groups", "expert"), None),
            P("track", ("groups", "expert"), None),
            P("track", ("groups", "expert"), None),
            P("track", None),
            P("track", "expert", None, None),
            P("track", "expert", None, None),
            P("track", "expert", None, None),
        ),
        out_specs=P(("groups", "expert"), "track"),
        check_vma=False,
    )
```

profile of v0, /device:TPU:0, one launch (start us, length us, event | category | flops | bytes accessed | tf_op | source)
XLA Modules:
  0.0 106.9 jit_solution(606662109196445409)
XLA Ops:
  0.0 0.5 collective-permute-start.13
  0.5 0.5 collective-permute-start.15
  1.0 1.2 %copy-done.3 = bf16[1,256,2048]{2,1,0:T(8,128)(2,1)S(1)} copy-done((bf16[1,256,2048]{2,1,0:T(8,128)(2,1)S(1)}, bf16[1,256,2048]{2,1,0:T(8,128)(2,1)}, u32[]{:S(2)}) %copy-start.3) | copy-done | bytes 1048600
  2.2 0.1 shard_map.73
  2.4 4.5 %collective-permute-start.2 = (bf16[64,2048]{1,0:T(8,128)(2,1)S(1)}, bf16[64,2048]{1,0:T(8,128)(2,1)S(1)}, u32[]{:S(2)}, u32[]{:S(2)}) collective-permute-start(bf16[64,2048]{1,0:T(8,128)(2,1)S(1)} %get-tuple-element.35.refs_0_), channel_id=1, source_target_pairs={{0,4},{12,8},{1,5},{13,9},{2,6},{14,10},{3,7},{15,11},{16,20},{28,... | collective-permute-start | bytes 786440 | tf_op jit(solution)/shard_map/ppermute | solution.py:338
  6.9 0.7 copy-done.5
  7.5 0.7 copy-done.6
  8.2 1.6 %collective-permute-start.3 = (f32[4,256]{1,0:T(4,128)S(1)}, f32[4,256]{1,0:T(4,128)S(1)}, u32[]{:S(2)}, u32[]{:S(2)}) collective-permute-start(f32[4,256]{1,0:T(4,128)S(1)} %shard_map.74.refs_0_), channel_id=1, source_target_pairs={{0,2},{1,3},{2,0},{3,1},{4,6},{5,7},{6,4},{7,5},{8,10},{9,11},{10,... | collective-permute-start | bytes 12296 | tf_op jit(solution)/shard_map/ppermute | solution.py:79
  9.8 2.1 %collective-permute-done.3.refs_1_ = f32[4,256]{1,0:T(4,128)S(1)} collective-permute-done((f32[4,256]{1,0:T(4,128)S(1)}, f32[4,256]{1,0:T(4,128)S(1)}, u32[]{:S(2)}, u32[]{:S(2)}) %collective-permute-start.3) | collective-permute-done | bytes 4128 | tf_op jit(solution)/shard_map/ppermute | solution.py:79
  11.9 1.3 %collective-permute-start.1 = (bf16[64,2048]{1,0:T(8,128)(2,1)S(1)}, bf16[64,2048]{1,0:T(8,128)(2,1)S(1)}, u32[]{:S(2)}, u32[]{:S(2)}) collective-permute-start(bf16[64,2048]{1,0:T(8,128)(2,1)S(1)} %get-tuple-element.34.refs_0_), channel_id=1, source_target_pairs={{0,4},{12,8},{1,5},{13,9},{2,6},{14,10},{3,7},{15,11},{16,20},{28,... | collective-permute-start | bytes 786440 | tf_op jit(solution)/shard_map/ppermute | solution.py:338
  13.2 4.3 %collective-permute-start.5 = (bf16[64,2048]{1,0:T(8,128)(2,1)S(1)}, bf16[64,2048]{1,0:T(8,128)(2,1)S(1)}, u32[]{:S(2)}, u32[]{:S(2)}) collective-permute-start(bf16[64,2048]{1,0:T(8,128)(2,1)S(1)} %get-tuple-element.36.refs_0_), channel_id=1, source_target_pairs={{0,4},{12,8},{1,5},{13,9},{2,6},{14,10},{3,7},{15,11},{16,20},{28,... | collective-permute-start | bytes 786440 | tf_op jit(solution)/shard_map/ppermute | solution.py:338
  17.6 0.1 shard_map.75.refs_2_.refs_3_
  17.7 0.1 shard_map.76.refs_2_
  17.8 2.1 %collective-permute-done.1.refs_1_ = bf16[64,2048]{1,0:T(8,128)(2,1)S(1)} collective-permute-done((bf16[64,2048]{1,0:T(8,128)(2,1)S(1)}, bf16[64,2048]{1,0:T(8,128)(2,1)S(1)}, u32[]{:S(2)}, u32[]{:S(2)}) %collective-permute-start.1) | collective-permute-done | bytes 262176 | tf_op jit(solution)/shard_map/ppermute | solution.py:338
  19.9 0.7 collective-permute-start.6
  20.6 0.1 shard_map.77.refs_3_
  20.6 3.7 %collective-permute-done.5.refs_1_ = bf16[64,2048]{1,0:T(8,128)(2,1)S(1)} collective-permute-done((bf16[64,2048]{1,0:T(8,128)(2,1)S(1)}, bf16[64,2048]{1,0:T(8,128)(2,1)S(1)}, u32[]{:S(2)}, u32[]{:S(2)}) %collective-permute-start.5) | collective-permute-done | bytes 262176 | tf_op jit(solution)/shard_map/ppermute | solution.py:338
  24.3 0.7 collective-permute-start.4
  25.0 8.3 %collective-permute-start = (bf16[64,2048]{1,0:T(8,128)(2,1)S(1)}, bf16[64,2048]{1,0:T(8,128)(2,1)S(1)}, u32[]{:S(2)}, u32[]{:S(2)}) collective-permute-start(bf16[64,2048]{1,0:T(8,128)(2,1)S(1)} %get-tuple-element.33.refs_0_), channel_id=1, source_target_pairs={{0,4},{12,8},{1,5},{13,9},{2,6},{14,10},{3,7},{15,11},{16,20},{28,... | collective-permute-start | bytes 786440 | tf_op jit(solution)/shard_map/ppermute | solution.py:338
  33.2 0.1 shard_map.78.refs_2_.refs_0_
  33.4 1.3 %collective-permute-start.10 = (bf16[64,2048]{1,0:T(8,128)(2,1)S(1)}, bf16[64,2048]{1,0:T(8,128)(2,1)S(1)}, u32[]{:S(2)}, u32[]{:S(2)}) collective-permute-start(bf16[64,2048]{1,0:T(8,128)(2,1)S(1)} %shard_map.78.refs_2_.refs_0_), channel_id=1, source_target_pairs={{4,0},{8,12},{5,1},{9,13},{6,2},{10,14},{7,3},{11,15},{20,16},{24,... | collective-permute-start | bytes 786440 | tf_op jit(solution)/shard_map/ppermute | solution.py:354
  34.7 0.1 shard_map.79.refs_3_
  34.7 0.1 shard_map.80.refs_2_.refs_0_
  34.9 2.2 %collective-permute-done.refs_1_ = bf16[64,2048]{1,0:T(8,128)(2,1)S(1)} collective-permute-done((bf16[64,2048]{1,0:T(8,128)(2,1)S(1)}, bf16[64,2048]{1,0:T(8,128)(2,1)S(1)}, u32[]{:S(2)}, u32[]{:S(2)}) %collective-permute-start) | collective-permute-done | bytes 262176 | tf_op jit(solution)/shard_map/ppermute | solution.py:338
  37.1 0.1 shard_map.81.refs_2_
  37.2 0.7 collective-permute-start.7
  37.9 4.6 %collective-permute-done.10.refs_1_ = bf16[64,2048]{1,0:T(8,128)(2,1)S(1)} collective-permute-done((bf16[64,2048]{1,0:T(8,128)(2,1)S(1)}, bf16[64,2048]{1,0:T(8,128)(2,1)S(1)}, u32[]{:S(2)}, u32[]{:S(2)}) %collective-permute-start.10) | collective-permute-done | bytes 262176 | tf_op jit(solution)/shard_map/ppermute | solution.py:354
  42.5 0.7 collective-permute-start.9
  43.2 1.3 %collective-permute-start.8 = (bf16[64,2048]{1,0:T(8,128)(2,1)S(1)}, bf16[64,2048]{1,0:T(8,128)(2,1)S(1)}, u32[]{:S(2)}, u32[]{:S(2)}) collective-permute-start(bf16[64,2048]{1,0:T(8,128)(2,1)S(1)} %shard_map.80.refs_2_.refs_0_), channel_id=1, source_target_pairs={{4,0},{8,12},{5,1},{9,13},{6,2},{10,14},{7,3},{11,15},{20,16},{24,... | collective-permute-start | bytes 786440 | tf_op jit(solution)/shard_map/ppermute | solution.py:354
  44.5 1.6 %collective-permute-start.17 = (bf16[64,2048]{1,0:T(8,128)(2,1)S(1)}, bf16[64,2048]{1,0:T(8,128)(2,1)S(1)}, u32[]{:S(2)}, u32[]{:S(2)}) collective-permute-start(bf16[64,2048]{1,0:T(8,128)(2,1)S(1)} %shard_map.82.refs_3_.refs_0_.refs_2_), channel_id=1, source_target_pairs={{0,2},{1,3},{2,0},{3,1},{4,6},{5,7},{6,4},{7,5},{8,10},{9,11},{10,... | collective-permute-start | bytes 786440 | tf_op jit(solution)/shard_map/ppermute | solution.py:318
  46.1 0.1 shard_map.83.refs_2_.refs_0_
  46.2 11.9 %collective-permute-done.8.refs_1_ = bf16[64,2048]{1,0:T(8,128)(2,1)S(1)} collective-permute-done((bf16[64,2048]{1,0:T(8,128)(2,1)S(1)}, bf16[64,2048]{1,0:T(8,128)(2,1)S(1)}, u32[]{:S(2)}, u32[]{:S(2)}) %collective-permute-start.8) | collective-permute-done | bytes 262176 | tf_op jit(solution)/shard_map/ppermute | solution.py:354
  58.0 1.3 %collective-permute-start.16 = (bf16[64,2048]{1,0:T(8,128)(2,1)S(1)}, bf16[64,2048]{1,0:T(8,128)(2,1)S(1)}, u32[]{:S(2)}, u32[]{:S(2)}) collective-permute-start(bf16[64,2048]{1,0:T(8,128)(2,1)S(1)} %shard_map.83.refs_2_.refs_0_), channel_id=1, source_target_pairs={{4,0},{8,12},{5,1},{9,13},{6,2},{10,14},{7,3},{11,15},{20,16},{24,... | collective-permute-start | bytes 786440 | tf_op jit(solution)/shard_map/ppermute | solution.py:354
  59.4 0.1 shard_map.85.refs_10_.refs_0_
  59.5 1.6 %collective-permute-start.12 = (bf16[64,2048]{1,0:T(8,128)(2,1)S(1)}, bf16[64,2048]{1,0:T(8,128)(2,1)S(1)}, u32[]{:S(2)}, u32[]{:S(2)}) collective-permute-start(bf16[64,2048]{1,0:T(8,128)(2,1)S(1)} %shard_map.84.refs_3_.refs_0_.refs_2_), channel_id=1, source_target_pairs={{0,2},{1,3},{2,0},{3,1},{4,6},{5,7},{6,4},{7,5},{8,10},{9,11},{10,... | collective-permute-start | bytes 786440 | tf_op jit(solution)/shard_map/ppermute | solution.py:318
  61.0 1.5 %collective-permute-start.11 = (bf16[64,2048]{1,0:T(8,128)(2,1)S(1)}, bf16[64,2048]{1,0:T(8,128)(2,1)S(1)}, u32[]{:S(2)}, u32[]{:S(2)}) collective-permute-start(bf16[64,2048]{1,0:T(8,128)(2,1)S(1)} %shard_map.85.refs_10_.refs_0_), channel_id=1, source_target_pairs={{4,0},{8,12},{5,1},{9,13},{6,2},{10,14},{7,3},{11,15},{20,16},{24,... | collective-permute-start | bytes 786440 | tf_op jit(solution)/shard_map/ppermute | solution.py:354
  62.6 2.9 %shard_map.86 = (f32[128,1024]{1,0:T(8,128)S(1)}, bf16[128,1024]{1,0:T(8,128)(2,1)S(1)}) custom-call(bf16[64,2048]{1,0:T(8,128)(2,1)S(1)} %shard_map.82.refs_3_.refs_0_.refs_2_, bf16[64,2048]{1,0:T(8,128)(2,1)S(1)} %collective-permute-done.17.refs_1_, f32[1,2048]{1,0:T(1,128)S(1)} %copy-done.4, f32[2,256,8]{2,1,0:T(8,128)S(1)} %shard_map.75.refs_2_.refs_3_, ...), custom_call_target="tpu_custom_call" | custom-call | tf_op jit(solution)/shard_map/pallas_call | solution.py:100
  65.5 2.8 %collective-permute-done.16.refs_1_ = bf16[64,2048]{1,0:T(8,128)(2,1)S(1)} collective-permute-done((bf16[64,2048]{1,0:T(8,128)(2,1)S(1)}, bf16[64,2048]{1,0:T(8,128)(2,1)S(1)}, u32[]{:S(2)}, u32[]{:S(2)}) %collective-permute-start.16) | collective-permute-done | bytes 262176 | tf_op jit(solution)/shard_map/ppermute | solution.py:354
  68.4 1.4 %collective-permute-start.20 = (bf16[64,2048]{1,0:T(8,128)(2,1)S(1)}, bf16[64,2048]{1,0:T(8,128)(2,1)S(1)}, u32[]{:S(2)}, u32[]{:S(2)}) collective-permute-start(bf16[64,2048]{1,0:T(8,128)(2,1)S(1)} %shard_map.87.refs_10_.refs_0_.refs_2_), channel_id=1, source_target_pairs={{0,2},{1,3},{2,0},{3,1},{4,6},{5,7},{6,4},{7,5},{8,10},{9,11},{10,... | collective-permute-start | bytes 786440 | tf_op jit(solution)/shard_map/ppermute | solution.py:318
  69.7 2.9 %shard_map.88 = (f32[128,1024]{1,0:T(8,128)S(1)}, bf16[128,1024]{1,0:T(8,128)(2,1)S(1)}) custom-call(bf16[64,2048]{1,0:T(8,128)(2,1)S(1)} %shard_map.84.refs_3_.refs_0_.refs_2_, bf16[64,2048]{1,0:T(8,128)(2,1)S(1)} %collective-permute-done.12.refs_1_, f32[1,2048]{1,0:T(1,128)S(1)} %copy-done.4, f32[2,256,8]{2,1,0:T(8,128)S(1)} %shard_map.75.refs_2_.refs_3_, ...), custom_call_target="tpu_custom_call" | custom-call | tf_op jit(solution)/shard_map/pallas_call | solution.py:100
  72.6 0.8 collective-permute-done.11.refs_1_
  73.5 1.0 collective-permute-start.18
  74.4 1.1 collective-permute-start.24
  75.5 2.1 %collective-permute-done.20.refs_1_ = bf16[64,2048]{1,0:T(8,128)(2,1)S(1)} collective-permute-done((bf16[64,2048]{1,0:T(8,128)(2,1)S(1)}, bf16[64,2048]{1,0:T(8,128)(2,1)S(1)}, u32[]{:S(2)}, u32[]{:S(2)}) %collective-permute-start.20) | collective-permute-done | bytes 262176 | tf_op jit(solution)/shard_map/ppermute | solution.py:318
  77.6 2.9 %shard_map.90 = (f32[64,2048]{1,0:T(8,128)S(1)}, bf16[64,2048]{1,0:T(8,128)(2,1)S(1)}) custom-call(bf16[64,2048]{1,0:T(8,128)(2,1)S(1)} %shard_map.87.refs_10_.refs_0_.refs_2_, bf16[64,2048]{1,0:T(8,128)(2,1)S(1)} %collective-permute-done.20.refs_1_, f32[1,2048]{1,0:T(1,128)S(1)} %copy-done.4, f32[2,256,8]{2,1,0:T(8,128)S(1)} %shard_map.75.refs_2_.refs_3_, ...), custom_call_target="tpu_custom_call" | custom-call | tf_op jit(solution)/shard_map/pallas_call | solution.py:100
  80.5 1.0 collective-permute-start.23
  81.5 0.1 shard_map.91
  81.6 1.1 %collective-permute-done.18.refs_1_ = bf16[64,2048]{1,0:T(8,128)(2,1)S(1)} collective-permute-done((bf16[64,2048]{1,0:T(8,128)(2,1)S(1)}, bf16[64,2048]{1,0:T(8,128)(2,1)S(1)}, u32[]{:S(2)}, u32[]{:S(2)}) %collective-permute-start.18) | collective-permute-done | bytes 262176 | tf_op jit(solution)/shard_map/ppermute | solution.py:318
  82.6 2.9 %shard_map.92 = (f32[64,2048]{1,0:T(8,128)S(1)}, bf16[64,2048]{1,0:T(8,128)(2,1)S(1)}) custom-call(bf16[64,2048]{1,0:T(8,128)(2,1)S(1)} %shard_map.89.refs_10_.refs_0_.refs_2_, bf16[64,2048]{1,0:T(8,128)(2,1)S(1)} %collective-permute-done.18.refs_1_, f32[1,2048]{1,0:T(1,128)S(1)} %copy-done.4, f32[2,256,8]{2,1,0:T(8,128)S(1)} %shard_map.75.refs_2_.refs_3_, ...), custom_call_target="tpu_custom_call" | custom-call | tf_op jit(solution)/shard_map/pallas_call | solution.py:100
  85.6 0.6 collective-permute-start.21
  86.2 2.2 %collective-permute-start.22 = (bf16[128,512]{1,0:T(8,128)(2,1)S(1)}, bf16[128,512]{1,0:T(8,128)(2,1)S(1)}, u32[]{:S(2)}, u32[]{:S(2)}) collective-permute-start(bf16[128,512]{1,0:T(8,128)(2,1)S(1)} %get-tuple-element.41.refs_10_), channel_id=1, source_target_pairs={{0,8},{4,12},{8,0},{12,4},{1,9},{5,13},{9,1},{13,5},{2,10},{6,14},... | collective-permute-start | bytes 393224 | tf_op jit(solution)/shard_map/ppermute | solution.py:318
  88.4 0.8 collective-permute-start.27
  89.3 1.1 %collective-permute-start.26 = (bf16[64,1024]{1,0:T(8,128)(2,1)S(1)}, bf16[64,1024]{1,0:T(8,128)(2,1)S(1)}, u32[]{:S(2)}, u32[]{:S(2)}) collective-permute-start(bf16[64,1024]{1,0:T(8,128)(2,1)S(1)} %get-tuple-element.48.refs_2_), channel_id=1, source_target_pairs={{0,4},{4,0},{8,12},{12,8},{1,5},{5,1},{9,13},{13,9},{2,6},{6,2},{1... | collective-permute-start | bytes 393224 | tf_op jit(solution)/shard_map/ppermute | solution.py:318
  90.4 5.3 %collective-permute-done.22.refs_1_ = bf16[128,512]{1,0:T(8,128)(2,1)S(1)} collective-permute-done((bf16[128,512]{1,0:T(8,128)(2,1)S(1)}, bf16[128,512]{1,0:T(8,128)(2,1)S(1)}, u32[]{:S(2)}, u32[]{:S(2)}) %collective-permute-start.22) | collective-permute-done | bytes 131104 | tf_op jit(solution)/shard_map/ppermute | solution.py:318
  95.7 0.1 shard_map.96
  95.7 0.1 collective-permute-start.25
  95.8 1.6 %collective-permute-start.29 = (bf16[64,512]{1,0:T(8,128)(2,1)S(1)}, bf16[64,512]{1,0:T(8,128)(2,1)S(1)}, u32[]{:S(2)}, u32[]{:S(2)}) collective-permute-start(bf16[64,512]{1,0:T(8,128)(2,1)S(1)} %get-tuple-element.49.refs_2_), channel_id=1, source_target_pairs={{0,2},{1,3},{2,0},{3,1},{4,6},{5,7},{6,4},{7,5},{8,10},{9,11},{10,... | collective-permute-start | bytes 196616 | tf_op jit(solution)/shard_map/ppermute | solution.py:318
  97.5 2.9 %collective-permute-start.31 = (bf16[64,512]{1,0:T(8,128)(2,1)S(1)}, bf16[64,512]{1,0:T(8,128)(2,1)S(1)}, u32[]{:S(2)}, u32[]{:S(2)}) collective-permute-start(bf16[64,512]{1,0:T(8,128)(2,1)S(1)} %get-tuple-element.55.refs_2_), channel_id=1, source_target_pairs={{0,8},{4,12},{8,0},{12,4},{1,9},{5,13},{9,1},{13,5},{2,10},{6,14},... | collective-permute-start | bytes 196616 | tf_op jit(solution)/shard_map/ppermute | solution.py:318
  100.4 0.5 collective-permute-start.30
  100.9 0.8 collective-permute-start.28
  101.8 0.9 collective-permute-done.31.refs_1_
  102.7 1.9 %collective-permute-done.30.refs_1_ = bf16[64,512]{1,0:T(8,128)(2,1)S(1)} collective-permute-done((bf16[64,512]{1,0:T(8,128)(2,1)S(1)}, bf16[64,512]{1,0:T(8,128)(2,1)S(1)}, u32[]{:S(2)}, u32[]{:S(2)}) %collective-permute-start.30) | collective-permute-done | bytes 65568 | tf_op jit(solution)/shard_map/ppermute | solution.py:318
  104.7 1.5 %collective-permute-done.28.refs_1_ = bf16[64,512]{1,0:T(8,128)(2,1)S(1)} collective-permute-done((bf16[64,512]{1,0:T(8,128)(2,1)S(1)}, bf16[64,512]{1,0:T(8,128)(2,1)S(1)}, u32[]{:S(2)}, u32[]{:S(2)}) %collective-permute-start.28) | collective-permute-done | bytes 65568 | tf_op jit(solution)/shard_map/ppermute | solution.py:318
  106.2 0.7 shard_map.103
  (45 shorter events, 0.6 us)
Async XLA Ops:
  0.0 61.0 %collective-permute-start.13 = (bf16[2048,768]{1,0:T(8,128)(2,1)}, bf16[2048,768]{1,0:T(8,128)(2,1)S(1)}, u32[]{:S(2)}, u32[]{:S(2)}) collective-permute-start(bf16[2048,768]{1,0:T(8,128)(2,1)} %bitcast.10), channel_id=1, source_target_pairs={{0,1},{1,0},{2,3},{3,2},{4,5},{5,4},{6,7},{7,6},{8,9},{9,8},{10,11... | collective-permute-start | bytes 9437192 | tf_op jit(solution)/shard_map/ppermute | solution.py:79
  0.5 62.0 %collective-permute-start.14 = (bf16[2048,768]{1,0:T(8,128)(2,1)}, bf16[2048,768]{1,0:T(8,128)(2,1)S(1)}, u32[]{:S(2)}, u32[]{:S(2)}) collective-permute-start(bf16[2048,768]{1,0:T(8,128)(2,1)} %bitcast.15), channel_id=1, source_target_pairs={{0,1},{1,0},{2,3},{3,2},{4,5},{5,4},{6,7},{7,6},{8,9},{9,8},{10,11... | collective-permute-start | bytes 9437192 | tf_op jit(solution)/shard_map/ppermute | solution.py:79
  0.5 62.0 %collective-permute-start.15 = (bf16[768,2048]{1,0:T(8,128)(2,1)}, bf16[768,2048]{1,0:T(8,128)(2,1)S(1)}, u32[]{:S(2)}, u32[]{:S(2)}) collective-permute-start(bf16[768,2048]{1,0:T(8,128)(2,1)} %bitcast.20), channel_id=1, source_target_pairs={{0,1},{1,0},{2,3},{3,2},{4,5},{5,4},{6,7},{7,6},{8,9},{9,8},{10,11... | collective-permute-start | bytes 9437192 | tf_op jit(solution)/shard_map/ppermute | solution.py:79
  1.0 1.2 %copy-start.3 = (bf16[1,256,2048]{2,1,0:T(8,128)(2,1)S(1)}, bf16[1,256,2048]{2,1,0:T(8,128)(2,1)}, u32[]{:S(2)}) copy-start(bf16[1,256,2048]{2,1,0:T(8,128)(2,1)} %param.7) | copy-start | bytes 3145732
  2.4 10.9 %collective-permute-start.2 = (bf16[64,2048]{1,0:T(8,128)(2,1)S(1)}, bf16[64,2048]{1,0:T(8,128)(2,1)S(1)}, u32[]{:S(2)}, u32[]{:S(2)}) collective-permute-start(bf16[64,2048]{1,0:T(8,128)(2,1)S(1)} %get-tuple-element.35.refs_0_), channel_id=1, source_target_pairs={{0,4},{12,8},{1,5},{13,9},{2,6},{14,10},{3,7},{15,11},{16,20},{28,... | collective-permute-start | bytes 786440 | tf_op jit(solution)/shard_map/ppermute | solution.py:338
  6.8 0.7 copy-start.5
  7.5 0.7 copy-start.6
  8.2 3.7 %collective-permute-start.3 = (f32[4,256]{1,0:T(4,128)S(1)}, f32[4,256]{1,0:T(4,128)S(1)}, u32[]{:S(2)}, u32[]{:S(2)}) collective-permute-start(f32[4,256]{1,0:T(4,128)S(1)} %shard_map.74.refs_0_), channel_id=1, source_target_pairs={{0,2},{1,3},{2,0},{3,1},{4,6},{5,7},{6,4},{7,5},{8,10},{9,11},{10,... | collective-permute-start | bytes 12296 | tf_op jit(solution)/shard_map/ppermute | solution.py:79
  11.9 8.0 %collective-permute-start.1 = (bf16[64,2048]{1,0:T(8,128)(2,1)S(1)}, bf16[64,2048]{1,0:T(8,128)(2,1)S(1)}, u32[]{:S(2)}, u32[]{:S(2)}) collective-permute-start(bf16[64,2048]{1,0:T(8,128)(2,1)S(1)} %get-tuple-element.34.refs_0_), channel_id=1, source_target_pairs={{0,4},{12,8},{1,5},{13,9},{2,6},{14,10},{3,7},{15,11},{16,20},{28,... | collective-permute-start | bytes 786440 | tf_op jit(solution)/shard_map/ppermute | solution.py:338
  13.2 11.1 %collective-permute-start.5 = (bf16[64,2048]{1,0:T(8,128)(2,1)S(1)}, bf16[64,2048]{1,0:T(8,128)(2,1)S(1)}, u32[]{:S(2)}, u32[]{:S(2)}) collective-permute-start(bf16[64,2048]{1,0:T(8,128)(2,1)S(1)} %get-tuple-element.36.refs_0_), channel_id=1, source_target_pairs={{0,4},{12,8},{1,5},{13,9},{2,6},{14,10},{3,7},{15,11},{16,20},{28,... | collective-permute-start | bytes 786440 | tf_op jit(solution)/shard_map/ppermute | solution.py:338
  19.9 5.1 %collective-permute-start.6 = (bf16[64,2048]{1,0:T(8,128)(2,1)S(1)}, bf16[64,2048]{1,0:T(8,128)(2,1)S(1)}, u32[]{:S(2)}, u32[]{:S(2)}) collective-permute-start(bf16[64,2048]{1,0:T(8,128)(2,1)S(1)} %shard_map.76.refs_2_), channel_id=1, source_target_pairs={{4,8},{8,4},{5,9},{9,5},{6,10},{10,6},{7,11},{11,7},{20,24},{24,20... | collective-permute-start | bytes 786440 | tf_op jit(solution)/shard_map/ppermute | solution.py:346
  20.5 42.0 %copy-start.4 = (f32[1,2048]{1,0:T(1,128)S(1)}, f32[1,2048]{1,0:T(1,128)}, u32[]{:S(2)}) copy-start(f32[1,2048]{1,0:T(1,128)} %refs_2_.7) | copy-start | bytes 24580
  24.3 9.1 %collective-permute-start.4 = (bf16[64,2048]{1,0:T(8,128)(2,1)S(1)}, bf16[64,2048]{1,0:T(8,128)(2,1)S(1)}, u32[]{:S(2)}, u32[]{:S(2)}) collective-permute-start(bf16[64,2048]{1,0:T(8,128)(2,1)S(1)} %shard_map.77.refs_3_), channel_id=1, source_target_pairs={{4,8},{8,4},{5,9},{9,5},{6,10},{10,6},{7,11},{11,7},{20,24},{24,20... | collective-permute-start | bytes 786440 | tf_op jit(solution)/shard_map/ppermute | solution.py:346
  25.0 37.6 %copy-start.2 = (bf16[1,1,768,2048]{3,2,1,0:T(8,128)(2,1)S(1)}, bf16[1,1,768,2048]{3,2,1,0:T(8,128)(2,1)}, u32[]{:S(2)}) copy-start(bf16[1,1,768,2048]{3,2,1,0:T(8,128)(2,1)} %param.13) | copy-start | bytes 9437188
  25.0 12.1 %collective-permute-start = (bf16[64,2048]{1,0:T(8,128)(2,1)S(1)}, bf16[64,2048]{1,0:T(8,128)(2,1)S(1)}, u32[]{:S(2)}, u32[]{:S(2)}) collective-permute-start(bf16[64,2048]{1,0:T(8,128)(2,1)S(1)} %get-tuple-element.33.refs_0_), channel_id=1, source_target_pairs={{0,4},{12,8},{1,5},{13,9},{2,6},{14,10},{3,7},{15,11},{16,20},{28,... | collective-permute-start | bytes 786440 | tf_op jit(solution)/shard_map/ppermute | solution.py:338
  33.4 9.1 %collective-permute-start.10 = (bf16[64,2048]{1,0:T(8,128)(2,1)S(1)}, bf16[64,2048]{1,0:T(8,128)(2,1)S(1)}, u32[]{:S(2)}, u32[]{:S(2)}) collective-permute-start(bf16[64,2048]{1,0:T(8,128)(2,1)S(1)} %shard_map.78.refs_2_.refs_0_), channel_id=1, source_target_pairs={{4,0},{8,12},{5,1},{9,13},{6,2},{10,14},{7,3},{11,15},{20,16},{24,... | collective-permute-start | bytes 786440 | tf_op jit(solution)/shard_map/ppermute | solution.py:354
  34.7 27.8 %copy-start.1 = (bf16[1,1,2048,768]{3,2,1,0:T(8,128)(2,1)S(1)}, bf16[1,1,2048,768]{3,2,1,0:T(8,128)(2,1)}, u32[]{:S(2)}) copy-start(bf16[1,1,2048,768]{3,2,1,0:T(8,128)(2,1)} %param.12) | copy-start | bytes 9437188
  34.9 27.7 %copy-start = (bf16[1,1,2048,768]{3,2,1,0:T(8,128)(2,1)S(1)}, bf16[1,1,2048,768]{3,2,1,0:T(8,128)(2,1)}, u32[]{:S(2)}) copy-start(bf16[1,1,2048,768]{3,2,1,0:T(8,128)(2,1)} %param.11) | copy-start | bytes 9437188
  37.2 6.0 %collective-permute-start.7 = (bf16[64,2048]{1,0:T(8,128)(2,1)S(1)}, bf16[64,2048]{1,0:T(8,128)(2,1)S(1)}, u32[]{:S(2)}, u32[]{:S(2)}) collective-permute-start(bf16[64,2048]{1,0:T(8,128)(2,1)S(1)} %shard_map.81.refs_2_), channel_id=1, source_target_pairs={{4,8},{8,4},{5,9},{9,5},{6,10},{10,6},{7,11},{11,7},{20,24},{24,20... | collective-permute-start | bytes 786440 | tf_op jit(solution)/shard_map/ppermute | solution.py:346
  42.5 2.0 %collective-permute-start.9 = (bf16[64,2048]{1,0:T(8,128)(2,1)S(1)}, bf16[64,2048]{1,0:T(8,128)(2,1)S(1)}, u32[]{:S(2)}, u32[]{:S(2)}) collective-permute-start(bf16[64,2048]{1,0:T(8,128)(2,1)S(1)} %shard_map.79.refs_3_), channel_id=1, source_target_pairs={{4,8},{8,4},{5,9},{9,5},{6,10},{10,6},{7,11},{11,7},{20,24},{24,20... | collective-permute-start | bytes 786440 | tf_op jit(solution)/shard_map/ppermute | solution.py:346
  43.2 14.9 %collective-permute-start.8 = (bf16[64,2048]{1,0:T(8,128)(2,1)S(1)}, bf16[64,2048]{1,0:T(8,128)(2,1)S(1)}, u32[]{:S(2)}, u32[]{:S(2)}) collective-permute-start(bf16[64,2048]{1,0:T(8,128)(2,1)S(1)} %shard_map.80.refs_2_.refs_0_), channel_id=1, source_target_pairs={{4,0},{8,12},{5,1},{9,13},{6,2},{10,14},{7,3},{11,15},{20,16},{24,... | collective-permute-start | bytes 786440 | tf_op jit(solution)/shard_map/ppermute | solution.py:354
  44.5 15.0 %collective-permute-start.17 = (bf16[64,2048]{1,0:T(8,128)(2,1)S(1)}, bf16[64,2048]{1,0:T(8,128)(2,1)S(1)}, u32[]{:S(2)}, u32[]{:S(2)}) collective-permute-start(bf16[64,2048]{1,0:T(8,128)(2,1)S(1)} %shard_map.82.refs_3_.refs_0_.refs_2_), channel_id=1, source_target_pairs={{0,2},{1,3},{2,0},{3,1},{4,6},{5,7},{6,4},{7,5},{8,10},{9,11},{10,... | collective-permute-start | bytes 786440 | tf_op jit(solution)/shard_map/ppermute | solution.py:318
  58.0 10.3 %collective-permute-start.16 = (bf16[64,2048]{1,0:T(8,128)(2,1)S(1)}, bf16[64,2048]{1,0:T(8,128)(2,1)S(1)}, u32[]{:S(2)}, u32[]{:S(2)}) collective-permute-start(bf16[64,2048]{1,0:T(8,128)(2,1)S(1)} %shard_map.83.refs_2_.refs_0_), channel_id=1, source_target_pairs={{4,0},{8,12},{5,1},{9,13},{6,2},{10,14},{7,3},{11,15},{20,16},{24,... | collective-permute-start | bytes 786440 | tf_op jit(solution)/shard_map/ppermute | solution.py:354
  59.5 10.2 %collective-permute-start.12 = (bf16[64,2048]{1,0:T(8,128)(2,1)S(1)}, bf16[64,2048]{1,0:T(8,128)(2,1)S(1)}, u32[]{:S(2)}, u32[]{:S(2)}) collective-permute-start(bf16[64,2048]{1,0:T(8,128)(2,1)S(1)} %shard_map.84.refs_3_.refs_0_.refs_2_), channel_id=1, source_target_pairs={{0,2},{1,3},{2,0},{3,1},{4,6},{5,7},{6,4},{7,5},{8,10},{9,11},{10,... | collective-permute-start | bytes 786440 | tf_op jit(solution)/shard_map/ppermute | solution.py:318
  61.0 12.4 %collective-permute-start.11 = (bf16[64,2048]{1,0:T(8,128)(2,1)S(1)}, bf16[64,2048]{1,0:T(8,128)(2,1)S(1)}, u32[]{:S(2)}, u32[]{:S(2)}) collective-permute-start(bf16[64,2048]{1,0:T(8,128)(2,1)S(1)} %shard_map.85.refs_10_.refs_0_), channel_id=1, source_target_pairs={{4,0},{8,12},{5,1},{9,13},{6,2},{10,14},{7,3},{11,15},{20,16},{24,... | collective-permute-start | bytes 786440 | tf_op jit(solution)/shard_map/ppermute | solution.py:354
  68.4 9.2 %collective-permute-start.20 = (bf16[64,2048]{1,0:T(8,128)(2,1)S(1)}, bf16[64,2048]{1,0:T(8,128)(2,1)S(1)}, u32[]{:S(2)}, u32[]{:S(2)}) collective-permute-start(bf16[64,2048]{1,0:T(8,128)(2,1)S(1)} %shard_map.87.refs_10_.refs_0_.refs_2_), channel_id=1, source_target_pairs={{0,2},{1,3},{2,0},{3,1},{4,6},{5,7},{6,4},{7,5},{8,10},{9,11},{10,... | collective-permute-start | bytes 786440 | tf_op jit(solution)/shard_map/ppermute | solution.py:318
  69.7 11.8 %collective-permute-start.19 = (bf16[128,1024]{1,0:T(8,128)(2,1)S(1)}, bf16[128,1024]{1,0:T(8,128)(2,1)S(1)}, u32[]{:S(2)}, u32[]{:S(2)}) collective-permute-start(bf16[128,1024]{1,0:T(8,128)(2,1)S(1)} %get-tuple-element.37.refs_2_), channel_id=1, source_target_pairs={{0,4},{4,0},{8,12},{12,8},{1,5},{5,1},{9,13},{13,9},{2,6},{6,2},{1... | collective-permute-start | bytes 786440 | tf_op jit(solution)/shard_map/ppermute | solution.py:318
  73.5 9.2 %collective-permute-start.18 = (bf16[64,2048]{1,0:T(8,128)(2,1)S(1)}, bf16[64,2048]{1,0:T(8,128)(2,1)S(1)}, u32[]{:S(2)}, u32[]{:S(2)}) collective-permute-start(bf16[64,2048]{1,0:T(8,128)(2,1)S(1)} %shard_map.89.refs_10_.refs_0_.refs_2_), channel_id=1, source_target_pairs={{0,2},{1,3},{2,0},{3,1},{4,6},{5,7},{6,4},{7,5},{8,10},{9,11},{10,... | collective-permute-start | bytes 786440 | tf_op jit(solution)/shard_map/ppermute | solution.py:318
  74.4 13.9 %collective-permute-start.24 = (bf16[128,1024]{1,0:T(8,128)(2,1)S(1)}, bf16[128,1024]{1,0:T(8,128)(2,1)S(1)}, u32[]{:S(2)}, u32[]{:S(2)}) collective-permute-start(bf16[128,1024]{1,0:T(8,128)(2,1)S(1)} %get-tuple-element.38.refs_2_), channel_id=1, source_target_pairs={{0,4},{4,0},{8,12},{12,8},{1,5},{5,1},{9,13},{13,9},{2,6},{6,2},{1... | collective-permute-start | bytes 786440 | tf_op jit(solution)/shard_map/ppermute | solution.py:318
  80.5 8.7 %collective-permute-start.23 = (bf16[64,2048]{1,0:T(8,128)(2,1)S(1)}, bf16[64,2048]{1,0:T(8,128)(2,1)S(1)}, u32[]{:S(2)}, u32[]{:S(2)}) collective-permute-start(bf16[64,2048]{1,0:T(8,128)(2,1)S(1)} %get-tuple-element.40.refs_2_), channel_id=1, source_target_pairs={{0,2},{1,3},{2,0},{3,1},{4,6},{5,7},{6,4},{7,5},{8,10},{9,11},{10,... | collective-permute-start | bytes 786440 | tf_op jit(solution)/shard_map/ppermute | solution.py:318
  85.6 10.1 %collective-permute-start.21 = (bf16[64,2048]{1,0:T(8,128)(2,1)S(1)}, bf16[64,2048]{1,0:T(8,128)(2,1)S(1)}, u32[]{:S(2)}, u32[]{:S(2)}) collective-permute-start(bf16[64,2048]{1,0:T(8,128)(2,1)S(1)} %get-tuple-element.43.refs_2_), channel_id=1, source_target_pairs={{0,2},{1,3},{2,0},{3,1},{4,6},{5,7},{6,4},{7,5},{8,10},{9,11},{10,... | collective-permute-start | bytes 786440 | tf_op jit(solution)/shard_map/ppermute | solution.py:318
  86.2 9.5 %collective-permute-start.22 = (bf16[128,512]{1,0:T(8,128)(2,1)S(1)}, bf16[128,512]{1,0:T(8,128)(2,1)S(1)}, u32[]{:S(2)}, u32[]{:S(2)}) collective-permute-start(bf16[128,512]{1,0:T(8,128)(2,1)S(1)} %get-tuple-element.41.refs_10_), channel_id=1, source_target_pairs={{0,8},{4,12},{8,0},{12,4},{1,9},{5,13},{9,1},{13,5},{2,10},{6,14},... | collective-permute-start | bytes 393224 | tf_op jit(solution)/shard_map/ppermute | solution.py:318
  88.4 8.9 %collective-permute-start.27 = (bf16[128,512]{1,0:T(8,128)(2,1)S(1)}, bf16[128,512]{1,0:T(8,128)(2,1)S(1)}, u32[]{:S(2)}, u32[]{:S(2)}) collective-permute-start(bf16[128,512]{1,0:T(8,128)(2,1)S(1)} %get-tuple-element.47.refs_2_), channel_id=1, source_target_pairs={{0,8},{4,12},{8,0},{12,4},{1,9},{5,13},{9,1},{13,5},{2,10},{6,14},... | collective-permute-start | bytes 393224 | tf_op jit(solution)/shard_map/ppermute | solution.py:318
  89.3 8.2 %collective-permute-start.26 = (bf16[64,1024]{1,0:T(8,128)(2,1)S(1)}, bf16[64,1024]{1,0:T(8,128)(2,1)S(1)}, u32[]{:S(2)}, u32[]{:S(2)}) collective-permute-start(bf16[64,1024]{1,0:T(8,128)(2,1)S(1)} %get-tuple-element.48.refs_2_), channel_id=1, source_target_pairs={{0,4},{4,0},{8,12},{12,8},{1,5},{5,1},{9,13},{13,9},{2,6},{6,2},{1... | collective-permute-start | bytes 393224 | tf_op jit(solution)/shard_map/ppermute | solution.py:318
  95.7 5.2 %collective-permute-start.25 = (bf16[64,1024]{1,0:T(8,128)(2,1)S(1)}, bf16[64,1024]{1,0:T(8,128)(2,1)S(1)}, u32[]{:S(2)}, u32[]{:S(2)}) collective-permute-start(bf16[64,1024]{1,0:T(8,128)(2,1)S(1)} %get-tuple-element.51.refs_2_), channel_id=1, source_target_pairs={{0,4},{4,0},{8,12},{12,8},{1,5},{5,1},{9,13},{13,9},{2,6},{6,2},{1... | collective-permute-start | bytes 393224 | tf_op jit(solution)/shard_map/ppermute | solution.py:318
  95.8 5.9 %collective-permute-start.29 = (bf16[64,512]{1,0:T(8,128)(2,1)S(1)}, bf16[64,512]{1,0:T(8,128)(2,1)S(1)}, u32[]{:S(2)}, u32[]{:S(2)}) collective-permute-start(bf16[64,512]{1,0:T(8,128)(2,1)S(1)} %get-tuple-element.49.refs_2_), channel_id=1, source_target_pairs={{0,2},{1,3},{2,0},{3,1},{4,6},{5,7},{6,4},{7,5},{8,10},{9,11},{10,... | collective-permute-start | bytes 196616 | tf_op jit(solution)/shard_map/ppermute | solution.py:318
  97.5 5.2 %collective-permute-start.31 = (bf16[64,512]{1,0:T(8,128)(2,1)S(1)}, bf16[64,512]{1,0:T(8,128)(2,1)S(1)}, u32[]{:S(2)}, u32[]{:S(2)}) collective-permute-start(bf16[64,512]{1,0:T(8,128)(2,1)S(1)} %get-tuple-element.55.refs_2_), channel_id=1, source_target_pairs={{0,8},{4,12},{8,0},{12,4},{1,9},{5,13},{9,1},{13,5},{2,10},{6,14},... | collective-permute-start | bytes 196616 | tf_op jit(solution)/shard_map/ppermute | solution.py:318
  100.4 4.3 %collective-permute-start.30 = (bf16[64,512]{1,0:T(8,128)(2,1)S(1)}, bf16[64,512]{1,0:T(8,128)(2,1)S(1)}, u32[]{:S(2)}, u32[]{:S(2)}) collective-permute-start(bf16[64,512]{1,0:T(8,128)(2,1)S(1)} %get-tuple-element.54.refs_2_), channel_id=1, source_target_pairs={{0,2},{1,3},{2,0},{3,1},{4,6},{5,7},{6,4},{7,5},{8,10},{9,11},{10,... | collective-permute-start | bytes 196616 | tf_op jit(solution)/shard_map/ppermute | solution.py:318
  100.9 5.2 %collective-permute-start.28 = (bf16[64,512]{1,0:T(8,128)(2,1)S(1)}, bf16[64,512]{1,0:T(8,128)(2,1)S(1)}, u32[]{:S(2)}, u32[]{:S(2)}) collective-permute-start(bf16[64,512]{1,0:T(8,128)(2,1)S(1)} %get-tuple-element.57.refs_3_), channel_id=1, source_target_pairs={{0,8},{4,12},{8,0},{12,4},{1,9},{5,13},{9,1},{13,5},{2,10},{6,14},... | collective-permute-start | bytes 196616 | tf_op jit(solution)/shard_map/ppermute | solution.py:318
where the time goes:
time: 107 us
  starting transfers between devices  47 us (44%)
  waiting for transfers between devices  43 us (40%)
  Pallas kernels  13.9 us (13%)
  local copies, waits for them, and re-layouts  2.61 us (2%)
    ppermute x4, waiting for transfers between devices, spread(): st['came'] = lax.ppermute(st['total'], 'track', outward(step))  20.1 us
    ppermute x4, starting transfers between devices, begin(): lax.ppermute(own, 'track', inward(0) if middle > 1 else across)  18.4 us
    ppermute x16, starting transfers between devices, trade(): lax.ppermute(value, axis, [(i, i ^ bit) for i in range(lax.axis_size(axis...  18 us
    pallas_call x31, Pallas kernels, call(): pl.pallas_call(kernel, out_shape=outs, in_specs=[space] * len(ins) + [ANY...  13.9 us
    ppermute x16, waiting for transfers between devices, trade(): lax.ppermute(value, axis, [(i, i ^ bit) for i in range(lax.axis_size(axis...  12.8 us
    ppermute x4, waiting for transfers between devices, begin(): lax.ppermute(own, 'track', inward(0) if middle > 1 else across)  7.98 us
    ppermute x4, starting transfers between devices, spread(): st['came'] = lax.ppermute(st['total'], 'track', outward(step))  5.33 us
    ppermute x4, starting transfers between devices, gather(): st['came'] = lax.ppermute(total, 'track', link)  2.67 us
  transfers between devices with their start and end apart: 32, of which 14 were waited for; matrix products, arithmetic and copies ran while one was open for 0% of the time, Pallas kernels for 12%

commit v1 on v0

--- a/solution.py
+++ b/solution.py
@@ -8,7 +8,9 @@
 from jax.sharding import PartitionSpec as P
 
 CHUNKS = (1, 1, 1, 1)
-HOP, START, WIRE, EXPERT = 1.5, 2.2, 22.5, 12.0
+HOP, START, MIDDLE, WIRE, EXPERT = 2.5, 2.0, 0.0, 22.5, 16.0
+SLACK, OLDEST = 0.0, False
+TUNED = ()
 ROWS_FIRST = 2
 
 
@@ -273,11 +275,14 @@
     order = []
     while pending:
         now = max(now, min(ready[c] for c in pending))
-        c = max((c for c in pending if ready[c] <= now), key=left)
+        able = [c for c in pending if ready[c] <= now + SLACK]
+        c = min(able) if OLDEST else max(able, key=left)
+        now = max(now, ready[c])
         at = pending.pop(c)
         order.append((c, at))
-        now += START + (EXPERT * shares[c] if plans[c][at][0] is expert else 0.1)
+        now += EXPERT * shares[c] if plans[c][at][0] is expert else 0.1
         if at + 1 < len(plans[c]):
+            now += START + (MIDDLE if plans[c][at + 1][1][0] == "mid" else 0.0)
             launch(c, at + 1)
     return order
 
@@ -457,7 +462,10 @@
     shares = [size / tok_rows for size in sizes]
     for c in range(len(sizes)):
         begin(c)
-    for c, at in order_of(shares, plans, expert):
+    order = order_of(shares, plans, expert)
+    if sorted(order) == sorted(TUNED):
+        order = TUNED
+    for c, at in order:
         plans[c][at][0](c)
     return result[0]
 

time: 107 us -> 110 us (1.028)
  starting transfers between devices: 47 us -> 48.9 us
    ppermute x16, waiting for transfers between devices: 12.8 us -> 14.7 us  [trade(): lax.ppermute(value, axis, [(i, i ^ bit) for i in range(lax.axis_size(axis...]
    ppermute x16, starting transfers between devices: 18 us -> 19.9 us  [trade(): lax.ppermute(value, axis, [(i, i ^ bit) for i in range(lax.axis_size(axis...]
  transfers between devices with their start and end apart: 32 -> 32, of which waited for: 14 -> 13; matrix products, arithmetic and copies ran while one was open for 0% -> 0% of each run, Pallas kernels for 12% -> 12%
where the time goes in v1:
time: 110 us
  starting transfers between devices  48.9 us (44%)
  waiting for transfers between devices  44 us (40%)
  Pallas kernels  13.9 us (13%)
  local copies, waits for them, and re-layouts  2.61 us (2%)
    ppermute x16, starting transfers between devices, trade(): lax.ppermute(value, axis, [(i, i ^ bit) for i in range(lax.axis_size(axis...  19.9 us
    ppermute x4, waiting for transfers between devices, spread(): st['came'] = lax.ppermute(st['total'], 'track', outward(step))  19.2 us
    ppermute x4, starting transfers between devices, begin(): lax.ppermute(own, 'track', inward(0) if middle > 1 else across)  18.4 us
    ppermute x16, waiting for transfers between devices, trade(): lax.ppermute(value, axis, [(i, i ^ bit) for i in range(lax.axis_size(axis...  14.7 us
    pallas_call x31, Pallas kernels, call(): pl.pallas_call(kernel, out_shape=outs, in_specs=[space] * len(ins) + [ANY...  13.9 us
    ppermute x4, waiting for transfers between devices, begin(): lax.ppermute(own, 'track', inward(0) if middle > 1 else across)  7.98 us
    ppermute x4, starting transfers between devices, spread(): st['came'] = lax.ppermute(st['total'], 'track', outward(step))  5.34 us
    ppermute x4, starting transfers between devices, gather(): st['came'] = lax.ppermute(total, 'track', link)  2.67 us
  transfers between devices with their start and end apart: 32, of which 13 were waited for; matrix products, arithmetic and copies ran while one was open for 0% of the time, Pallas kernels for 12%

profile of v1, /device:TPU:0, one launch (start us, length us, event | category | flops | bytes accessed | tf_op | source)
XLA Modules:
  0.0 109.8 jit_solution(12380800094814087590)
XLA Ops:
  0.0 0.5 collective-permute-start.14
  0.5 0.5 collective-permute-start.16
  1.0 1.2 %copy-done.3 = bf16[1,256,2048]{2,1,0:T(8,128)(2,1)S(1)} copy-done((bf16[1,256,2048]{2,1,0:T(8,128)(2,1)S(1)}, bf16[1,256,2048]{2,1,0:T(8,128)(2,1)}, u32[]{:S(2)}) %copy-start.3) | copy-done | bytes 1048600
  2.2 0.1 shard_map.73
  2.4 4.5 %collective-permute-start.2 = (bf16[64,2048]{1,0:T(8,128)(2,1)S(1)}, bf16[64,2048]{1,0:T(8,128)(2,1)S(1)}, u32[]{:S(2)}, u32[]{:S(2)}) collective-permute-start(bf16[64,2048]{1,0:T(8,128)(2,1)S(1)} %get-tuple-element.35.refs_0_), channel_id=1, source_target_pairs={{0,4},{12,8},{1,5},{13,9},{2,6},{14,10},{3,7},{15,11},{16,20},{28,... | collective-permute-start | bytes 786440 | tf_op jit(solution)/shard_map/ppermute | solution.py:343
  6.9 0.7 copy-done.5
  7.5 0.7 copy-done.6
  8.2 1.6 %collective-permute-start.3 = (f32[4,256]{1,0:T(4,128)S(1)}, f32[4,256]{1,0:T(4,128)S(1)}, u32[]{:S(2)}, u32[]{:S(2)}) collective-permute-start(f32[4,256]{1,0:T(4,128)S(1)} %shard_map.74.refs_0_), channel_id=1, source_target_pairs={{0,2},{1,3},{2,0},{3,1},{4,6},{5,7},{6,4},{7,5},{8,10},{9,11},{10,... | collective-permute-start | bytes 12296 | tf_op jit(solution)/shard_map/ppermute | solution.py:81
  9.8 2.1 %collective-permute-done.3.refs_1_ = f32[4,256]{1,0:T(4,128)S(1)} collective-permute-done((f32[4,256]{1,0:T(4,128)S(1)}, f32[4,256]{1,0:T(4,128)S(1)}, u32[]{:S(2)}, u32[]{:S(2)}) %collective-permute-start.3) | collective-permute-done | bytes 4128 | tf_op jit(solution)/shard_map/ppermute | solution.py:81
  11.9 1.3 %collective-permute-start.1 = (bf16[64,2048]{1,0:T(8,128)(2,1)S(1)}, bf16[64,2048]{1,0:T(8,128)(2,1)S(1)}, u32[]{:S(2)}, u32[]{:S(2)}) collective-permute-start(bf16[64,2048]{1,0:T(8,128)(2,1)S(1)} %get-tuple-element.34.refs_0_), channel_id=1, source_target_pairs={{0,4},{12,8},{1,5},{13,9},{2,6},{14,10},{3,7},{15,11},{16,20},{28,... | collective-permute-start | bytes 786440 | tf_op jit(solution)/shard_map/ppermute | solution.py:343
  13.2 4.3 %collective-permute-start.5 = (bf16[64,2048]{1,0:T(8,128)(2,1)S(1)}, bf16[64,2048]{1,0:T(8,128)(2,1)S(1)}, u32[]{:S(2)}, u32[]{:S(2)}) collective-permute-start(bf16[64,2048]{1,0:T(8,128)(2,1)S(1)} %get-tuple-element.36.refs_0_), channel_id=1, source_target_pairs={{0,4},{12,8},{1,5},{13,9},{2,6},{14,10},{3,7},{15,11},{16,20},{28,... | collective-permute-start | bytes 786440 | tf_op jit(solution)/shard_map/ppermute | solution.py:343
  17.6 0.1 shard_map.75.refs_2_.refs_3_
  17.7 0.1 shard_map.76.refs_2_
  17.8 2.1 %collective-permute-done.1.refs_1_ = bf16[64,2048]{1,0:T(8,128)(2,1)S(1)} collective-permute-done((bf16[64,2048]{1,0:T(8,128)(2,1)S(1)}, bf16[64,2048]{1,0:T(8,128)(2,1)S(1)}, u32[]{:S(2)}, u32[]{:S(2)}) %collective-permute-start.1) | collective-permute-done | bytes 262176 | tf_op jit(solution)/shard_map/ppermute | solution.py:343
  19.9 0.7 collective-permute-start.6
  20.6 0.1 shard_map.77.refs_3_
  20.6 3.7 %collective-permute-done.5.refs_1_ = bf16[64,2048]{1,0:T(8,128)(2,1)S(1)} collective-permute-done((bf16[64,2048]{1,0:T(8,128)(2,1)S(1)}, bf16[64,2048]{1,0:T(8,128)(2,1)S(1)}, u32[]{:S(2)}, u32[]{:S(2)}) %collective-permute-start.5) | collective-permute-done | bytes 262176 | tf_op jit(solution)/shard_map/ppermute | solution.py:343
  24.3 0.7 collective-permute-start.4
  25.0 8.3 %collective-permute-start = (bf16[64,2048]{1,0:T(8,128)(2,1)S(1)}, bf16[64,2048]{1,0:T(8,128)(2,1)S(1)}, u32[]{:S(2)}, u32[]{:S(2)}) collective-permute-start(bf16[64,2048]{1,0:T(8,128)(2,1)S(1)} %get-tuple-element.33.refs_0_), channel_id=1, source_target_pairs={{0,4},{12,8},{1,5},{13,9},{2,6},{14,10},{3,7},{15,11},{16,20},{28,... | collective-permute-start | bytes 786440 | tf_op jit(solution)/shard_map/ppermute | solution.py:343
  33.2 0.1 shard_map.78.refs_2_.refs_0_
  33.4 1.3 %collective-permute-start.10 = (bf16[64,2048]{1,0:T(8,128)(2,1)S(1)}, bf16[64,2048]{1,0:T(8,128)(2,1)S(1)}, u32[]{:S(2)}, u32[]{:S(2)}) collective-permute-start(bf16[64,2048]{1,0:T(8,128)(2,1)S(1)} %shard_map.78.refs_2_.refs_0_), channel_id=1, source_target_pairs={{4,0},{8,12},{5,1},{9,13},{6,2},{10,14},{7,3},{11,15},{20,16},{24,... | collective-permute-start | bytes 786440 | tf_op jit(solution)/shard_map/ppermute | solution.py:359
  34.7 0.1 shard_map.79.refs_3_
  34.7 0.1 shard_map.80.refs_2_.refs_0_
  34.9 2.2 %collective-permute-done.refs_1_ = bf16[64,2048]{1,0:T(8,128)(2,1)S(1)} collective-permute-done((bf16[64,2048]{1,0:T(8,128)(2,1)S(1)}, bf16[64,2048]{1,0:T(8,128)(2,1)S(1)}, u32[]{:S(2)}, u32[]{:S(2)}) %collective-permute-start) | collective-permute-done | bytes 262176 | tf_op jit(solution)/shard_map/ppermute | solution.py:343
  37.2 0.7 collective-permute-start.7
  37.9 4.6 %collective-permute-done.10.refs_1_ = bf16[64,2048]{1,0:T(8,128)(2,1)S(1)} collective-permute-done((bf16[64,2048]{1,0:T(8,128)(2,1)S(1)}, bf16[64,2048]{1,0:T(8,128)(2,1)S(1)}, u32[]{:S(2)}, u32[]{:S(2)}) %collective-permute-start.10) | collective-permute-done | bytes 262176 | tf_op jit(solution)/shard_map/ppermute | solution.py:359
  42.5 0.7 collective-permute-start.9
  43.2 1.3 %collective-permute-start.8 = (bf16[64,2048]{1,0:T(8,128)(2,1)S(1)}, bf16[64,2048]{1,0:T(8,128)(2,1)S(1)}, u32[]{:S(2)}, u32[]{:S(2)}) collective-permute-start(bf16[64,2048]{1,0:T(8,128)(2,1)S(1)} %shard_map.80.refs_2_.refs_0_), channel_id=1, source_target_pairs={{4,0},{8,12},{5,1},{9,13},{6,2},{10,14},{7,3},{11,15},{20,16},{24,... | collective-permute-start | bytes 786440 | tf_op jit(solution)/shard_map/ppermute | solution.py:359
  44.5 1.6 %collective-permute-start.13 = (bf16[64,2048]{1,0:T(8,128)(2,1)S(1)}, bf16[64,2048]{1,0:T(8,128)(2,1)S(1)}, u32[]{:S(2)}, u32[]{:S(2)}) collective-permute-start(bf16[64,2048]{1,0:T(8,128)(2,1)S(1)} %shard_map.82.refs_3_.refs_0_.refs_2_), channel_id=1, source_target_pairs={{0,2},{1,3},{2,0},{3,1},{4,6},{5,7},{6,4},{7,5},{8,10},{9,11},{10,... | collective-permute-start | bytes 786440 | tf_op jit(solution)/shard_map/ppermute | solution.py:323
  46.1 0.1 shard_map.83.refs_2_.refs_0_
  46.2 11.9 %collective-permute-done.8.refs_1_ = bf16[64,2048]{1,0:T(8,128)(2,1)S(1)} collective-permute-done((bf16[64,2048]{1,0:T(8,128)(2,1)S(1)}, bf16[64,2048]{1,0:T(8,128)(2,1)S(1)}, u32[]{:S(2)}, u32[]{:S(2)}) %collective-permute-start.8) | collective-permute-done | bytes 262176 | tf_op jit(solution)/shard_map/ppermute | solution.py:359
  58.0 1.3 %collective-permute-start.12 = (bf16[64,2048]{1,0:T(8,128)(2,1)S(1)}, bf16[64,2048]{1,0:T(8,128)(2,1)S(1)}, u32[]{:S(2)}, u32[]{:S(2)}) collective-permute-start(bf16[64,2048]{1,0:T(8,128)(2,1)S(1)} %shard_map.83.refs_2_.refs_0_), channel_id=1, source_target_pairs={{4,0},{8,12},{5,1},{9,13},{6,2},{10,14},{7,3},{11,15},{20,16},{24,... | collective-permute-start | bytes 786440 | tf_op jit(solution)/shard_map/ppermute | solution.py:359
  59.4 0.1 shard_map.85.refs_10_.refs_0_
  59.5 1.5 %collective-permute-start.11 = (bf16[64,2048]{1,0:T(8,128)(2,1)S(1)}, bf16[64,2048]{1,0:T(8,128)(2,1)S(1)}, u32[]{:S(2)}, u32[]{:S(2)}) collective-permute-start(bf16[64,2048]{1,0:T(8,128)(2,1)S(1)} %shard_map.85.refs_10_.refs_0_), channel_id=1, source_target_pairs={{4,0},{8,12},{5,1},{9,13},{6,2},{10,14},{7,3},{11,15},{20,16},{24,... | collective-permute-start | bytes 786440 | tf_op jit(solution)/shard_map/ppermute | solution.py:359
  61.0 1.6 %collective-permute-start.20 = (bf16[64,2048]{1,0:T(8,128)(2,1)S(1)}, bf16[64,2048]{1,0:T(8,128)(2,1)S(1)}, u32[]{:S(2)}, u32[]{:S(2)}) collective-permute-start(bf16[64,2048]{1,0:T(8,128)(2,1)S(1)} %shard_map.84.refs_3_.refs_0_.refs_2_), channel_id=1, source_target_pairs={{0,2},{1,3},{2,0},{3,1},{4,6},{5,7},{6,4},{7,5},{8,10},{9,11},{10,... | collective-permute-start | bytes 786440 | tf_op jit(solution)/shard_map/ppermute | solution.py:323
  62.6 2.9 %shard_map.86 = (f32[128,1024]{1,0:T(8,128)S(1)}, bf16[128,1024]{1,0:T(8,128)(2,1)S(1)}) custom-call(bf16[64,2048]{1,0:T(8,128)(2,1)S(1)} %shard_map.82.refs_3_.refs_0_.refs_2_, bf16[64,2048]{1,0:T(8,128)(2,1)S(1)} %collective-permute-done.13.refs_1_, f32[1,2048]{1,0:T(1,128)S(1)} %copy-done.4, f32[2,256,8]{2,1,0:T(8,128)S(1)} %shard_map.75.refs_2_.refs_3_, ...), custom_call_target="tpu_custom_call" | custom-call | tf_op jit(solution)/shard_map/pallas_call | solution.py:102
  65.5 2.7 %collective-permute-start.19 = (bf16[128,1024]{1,0:T(8,128)(2,1)S(1)}, bf16[128,1024]{1,0:T(8,128)(2,1)S(1)}, u32[]{:S(2)}, u32[]{:S(2)}) collective-permute-start(bf16[128,1024]{1,0:T(8,128)(2,1)S(1)} %get-tuple-element.37.refs_2_), channel_id=1, source_target_pairs={{0,4},{4,0},{8,12},{12,8},{1,5},{5,1},{9,13},{13,9},{2,6},{6,2},{1... | collective-permute-start | bytes 786440 | tf_op jit(solution)/shard_map/ppermute | solution.py:323
  68.3 0.6 collective-permute-start.18
  68.9 2.7 %collective-permute-done.11.refs_1_ = bf16[64,2048]{1,0:T(8,128)(2,1)S(1)} collective-permute-done((bf16[64,2048]{1,0:T(8,128)(2,1)S(1)}, bf16[64,2048]{1,0:T(8,128)(2,1)S(1)}, u32[]{:S(2)}, u32[]{:S(2)}) %collective-permute-start.11) | collective-permute-done | bytes 262176 | tf_op jit(solution)/shard_map/ppermute | solution.py:359
  71.6 2.4 %collective-permute-start.17 = (bf16[64,2048]{1,0:T(8,128)(2,1)S(1)}, bf16[64,2048]{1,0:T(8,128)(2,1)S(1)}, u32[]{:S(2)}, u32[]{:S(2)}) collective-permute-start(bf16[64,2048]{1,0:T(8,128)(2,1)S(1)} %shard_map.88.refs_10_.refs_0_.refs_2_), channel_id=1, source_target_pairs={{0,2},{1,3},{2,0},{3,1},{4,6},{5,7},{6,4},{7,5},{8,10},{9,11},{10,... | collective-permute-start | bytes 786440 | tf_op jit(solution)/shard_map/ppermute | solution.py:323
  74.0 2.9 %shard_map.89 = (f32[128,1024]{1,0:T(8,128)S(1)}, bf16[128,1024]{1,0:T(8,128)(2,1)S(1)}) custom-call(bf16[64,2048]{1,0:T(8,128)(2,1)S(1)} %shard_map.84.refs_3_.refs_0_.refs_2_, bf16[64,2048]{1,0:T(8,128)(2,1)S(1)} %collective-permute-done.20.refs_1_, f32[1,2048]{1,0:T(1,128)S(1)} %copy-done.4, f32[2,256,8]{2,1,0:T(8,128)S(1)} %shard_map.75.refs_2_.refs_3_, ...), custom_call_target="tpu_custom_call" | custom-call | tf_op jit(solution)/shard_map/pallas_call | solution.py:102
  76.9 0.1 collective-permute-start.24
  77.0 0.1 shard_map.90
  77.1 2.9 %shard_map.91 = (f32[64,2048]{1,0:T(8,128)S(1)}, bf16[64,2048]{1,0:T(8,128)(2,1)S(1)}) custom-call(bf16[64,2048]{1,0:T(8,128)(2,1)S(1)} %shard_map.87.refs_2_.refs_0_, bf16[64,2048]{1,0:T(8,128)(2,1)S(1)} %collective-permute-done.18.refs_1_, f32[1,2048]{1,0:T(1,128)S(1)} %copy-done.4, f32[2,256,8]{2,1,0:T(8,128)S(1)} %shard_map.75.refs_2_.refs_3_, ...), custom_call_target="tpu_custom_call" | custom-call | tf_op jit(solution)/shard_map/pallas_call | solution.py:102
  80.0 0.6 collective-permute-start.22
  80.6 1.8 %collective-permute-done.17.refs_1_ = bf16[64,2048]{1,0:T(8,128)(2,1)S(1)} collective-permute-done((bf16[64,2048]{1,0:T(8,128)(2,1)S(1)}, bf16[64,2048]{1,0:T(8,128)(2,1)S(1)}, u32[]{:S(2)}, u32[]{:S(2)}) %collective-permute-start.17) | collective-permute-done | bytes 262176 | tf_op jit(solution)/shard_map/ppermute | solution.py:323
  82.5 2.9 %shard_map.92 = (f32[64,2048]{1,0:T(8,128)S(1)}, bf16[64,2048]{1,0:T(8,128)(2,1)S(1)}) custom-call(bf16[64,2048]{1,0:T(8,128)(2,1)S(1)} %shard_map.88.refs_10_.refs_0_.refs_2_, bf16[64,2048]{1,0:T(8,128)(2,1)S(1)} %collective-permute-done.17.refs_1_, f32[1,2048]{1,0:T(1,128)S(1)} %copy-done.4, f32[2,256,8]{2,1,0:T(8,128)S(1)} %shard_map.75.refs_2_.refs_3_, ...), custom_call_target="tpu_custom_call" | custom-call | tf_op jit(solution)/shard_map/pallas_call | solution.py:102
  85.4 0.9 collective-permute-start.21
  86.2 1.8 %collective-permute-start.23 = (bf16[128,512]{1,0:T(8,128)(2,1)S(1)}, bf16[128,512]{1,0:T(8,128)(2,1)S(1)}, u32[]{:S(2)}, u32[]{:S(2)}) collective-permute-start(bf16[128,512]{1,0:T(8,128)(2,1)S(1)} %get-tuple-element.40.refs_10_), channel_id=1, source_target_pairs={{0,8},{4,12},{8,0},{12,4},{1,9},{5,13},{9,1},{13,5},{2,10},{6,14},... | collective-permute-start | bytes 393224 | tf_op jit(solution)/shard_map/ppermute | solution.py:323
  88.1 1.2 %collective-permute-start.28 = (bf16[128,512]{1,0:T(8,128)(2,1)S(1)}, bf16[128,512]{1,0:T(8,128)(2,1)S(1)}, u32[]{:S(2)}, u32[]{:S(2)}) collective-permute-start(bf16[128,512]{1,0:T(8,128)(2,1)S(1)} %get-tuple-element.47.refs_2_), channel_id=1, source_target_pairs={{0,8},{4,12},{8,0},{12,4},{1,9},{5,13},{9,1},{13,5},{2,10},{6,14},... | collective-permute-start | bytes 393224 | tf_op jit(solution)/shard_map/ppermute | solution.py:323
  89.3 7.9 %collective-permute-done.23.refs_1_ = bf16[128,512]{1,0:T(8,128)(2,1)S(1)} collective-permute-done((bf16[128,512]{1,0:T(8,128)(2,1)S(1)}, bf16[128,512]{1,0:T(8,128)(2,1)S(1)}, u32[]{:S(2)}, u32[]{:S(2)}) %collective-permute-start.23) | collective-permute-done | bytes 131104 | tf_op jit(solution)/shard_map/ppermute | solution.py:323
  97.2 0.1 shard_map.95
  97.3 0.1 collective-permute-start.27
  97.4 0.1 shard_map.96
  97.5 2.1 %collective-permute-start.25 = (bf16[64,1024]{1,0:T(8,128)(2,1)S(1)}, bf16[64,1024]{1,0:T(8,128)(2,1)S(1)}, u32[]{:S(2)}, u32[]{:S(2)}) collective-permute-start(bf16[64,1024]{1,0:T(8,128)(2,1)S(1)} %get-tuple-element.51.refs_2_), channel_id=1, source_target_pairs={{0,4},{4,0},{8,12},{12,8},{1,5},{5,1},{9,13},{13,9},{2,6},{6,2},{1... | collective-permute-start | bytes 393224 | tf_op jit(solution)/shard_map/ppermute | solution.py:323
  99.5 0.2 collective-permute-start.26
  99.7 1.9 %collective-permute-start.30 = (bf16[64,512]{1,0:T(8,128)(2,1)S(1)}, bf16[64,512]{1,0:T(8,128)(2,1)S(1)}, u32[]{:S(2)}, u32[]{:S(2)}) collective-permute-start(bf16[64,512]{1,0:T(8,128)(2,1)S(1)} %get-tuple-element.55.refs_2_), channel_id=1, source_target_pairs={{0,2},{1,3},{2,0},{3,1},{4,6},{5,7},{6,4},{7,5},{8,10},{9,11},{10,... | collective-permute-start | bytes 196616 | tf_op jit(solution)/shard_map/ppermute | solution.py:323
  101.6 0.7 collective-permute-done.27.refs_1_
  102.4 0.7 collective-permute-start.31
  103.0 0.7 collective-permute-done.26.refs_1_
  103.9 1.6 %collective-permute-start.29 = (bf16[64,512]{1,0:T(8,128)(2,1)S(1)}, bf16[64,512]{1,0:T(8,128)(2,1)S(1)}, u32[]{:S(2)}, u32[]{:S(2)}) collective-permute-start(bf16[64,512]{1,0:T(8,128)(2,1)S(1)} %get-tuple-element.58.refs_3_), channel_id=1, source_target_pairs={{0,8},{4,12},{8,0},{12,4},{1,9},{5,13},{9,1},{13,5},{2,10},{6,14},... | collective-permute-start | bytes 196616 | tf_op jit(solution)/shard_map/ppermute | solution.py:323
  105.6 2.2 %collective-permute-done.31.refs_1_ = bf16[64,512]{1,0:T(8,128)(2,1)S(1)} collective-permute-done((bf16[64,512]{1,0:T(8,128)(2,1)S(1)}, bf16[64,512]{1,0:T(8,128)(2,1)S(1)}, u32[]{:S(2)}, u32[]{:S(2)}) %collective-permute-start.31) | collective-permute-done | bytes 65568 | tf_op jit(solution)/shard_map/ppermute | solution.py:323
  107.8 1.3 %collective-permute-done.29.refs_1_ = bf16[64,512]{1,0:T(8,128)(2,1)S(1)} collective-permute-done((bf16[64,512]{1,0:T(8,128)(2,1)S(1)}, bf16[64,512]{1,0:T(8,128)(2,1)S(1)}, u32[]{:S(2)}, u32[]{:S(2)}) %collective-permute-start.29) | collective-permute-done | bytes 65568 | tf_op jit(solution)/shard_map/ppermute | solution.py:323
  109.1 0.7 shard_map.103
  (45 shorter events, 0.6 us)
Async XLA Ops:
  0.0 61.0 %collective-permute-start.14 = (bf16[2048,768]{1,0:T(8,128)(2,1)}, bf16[2048,768]{1,0:T(8,128)(2,1)S(1)}, u32[]{:S(2)}, u32[]{:S(2)}) collective-permute-start(bf16[2048,768]{1,0:T(8,128)(2,1)} %bitcast.10), channel_id=1, source_target_pairs={{0,1},{1,0},{2,3},{3,2},{4,5},{5,4},{6,7},{7,6},{8,9},{9,8},{10,11... | collective-permute-start | bytes 9437192 | tf_op jit(solution)/shard_map/ppermute | solution.py:81
  0.5 62.0 %collective-permute-start.15 = (bf16[2048,768]{1,0:T(8,128)(2,1)}, bf16[2048,768]{1,0:T(8,128)(2,1)S(1)}, u32[]{:S(2)}, u32[]{:S(2)}) collective-permute-start(bf16[2048,768]{1,0:T(8,128)(2,1)} %bitcast.15), channel_id=1, source_target_pairs={{0,1},{1,0},{2,3},{3,2},{4,5},{5,4},{6,7},{7,6},{8,9},{9,8},{10,11... | collective-permute-start | bytes 9437192 | tf_op jit(solution)/shard_map/ppermute | solution.py:81
  0.5 62.0 %collective-permute-start.16 = (bf16[768,2048]{1,0:T(8,128)(2,1)}, bf16[768,2048]{1,0:T(8,128)(2,1)S(1)}, u32[]{:S(2)}, u32[]{:S(2)}) collective-permute-start(bf16[768,2048]{1,0:T(8,128)(2,1)} %bitcast.20), channel_id=1, source_target_pairs={{0,1},{1,0},{2,3},{3,2},{4,5},{5,4},{6,7},{7,6},{8,9},{9,8},{10,11... | collective-permute-start | bytes 9437192 | tf_op jit(solution)/shard_map/ppermute | solution.py:81
  1.0 1.2 %copy-start.3 = (bf16[1,256,2048]{2,1,0:T(8,128)(2,1)S(1)}, bf16[1,256,2048]{2,1,0:T(8,128)(2,1)}, u32[]{:S(2)}) copy-start(bf16[1,256,2048]{2,1,0:T(8,128)(2,1)} %param.7) | copy-start | bytes 3145732
  2.4 10.9 %collective-permute-start.2 = (bf16[64,2048]{1,0:T(8,128)(2,1)S(1)}, bf16[64,2048]{1,0:T(8,128)(2,1)S(1)}, u32[]{:S(2)}, u32[]{:S(2)}) collective-permute-start(bf16[64,2048]{1,0:T(8,128)(2,1)S(1)} %get-tuple-element.35.refs_0_), channel_id=1, source_target_pairs={{0,4},{12,8},{1,5},{13,9},{2,6},{14,10},{3,7},{15,11},{16,20},{28,... | collective-permute-start | bytes 786440 | tf_op jit(solution)/shard_map/ppermute | solution.py:343
  6.8 0.7 copy-start.5
  7.5 0.7 copy-start.6
  8.2 3.7 %collective-permute-start.3 = (f32[4,256]{1,0:T(4,128)S(1)}, f32[4,256]{1,0:T(4,128)S(1)}, u32[]{:S(2)}, u32[]{:S(2)}) collective-permute-start(f32[4,256]{1,0:T(4,128)S(1)} %shard_map.74.refs_0_), channel_id=1, source_target_pairs={{0,2},{1,3},{2,0},{3,1},{4,6},{5,7},{6,4},{7,5},{8,10},{9,11},{10,... | collective-permute-start | bytes 12296 | tf_op jit(solution)/shard_map/ppermute | solution.py:81
  11.9 8.0 %collective-permute-start.1 = (bf16[64,2048]{1,0:T(8,128)(2,1)S(1)}, bf16[64,2048]{1,0:T(8,128)(2,1)S(1)}, u32[]{:S(2)}, u32[]{:S(2)}) collective-permute-start(bf16[64,2048]{1,0:T(8,128)(2,1)S(1)} %get-tuple-element.34.refs_0_), channel_id=1, source_target_pairs={{0,4},{12,8},{1,5},{13,9},{2,6},{14,10},{3,7},{15,11},{16,20},{28,... | collective-permute-start | bytes 786440 | tf_op jit(solution)/shard_map/ppermute | solution.py:343
  13.2 11.1 %collective-permute-start.5 = (bf16[64,2048]{1,0:T(8,128)(2,1)S(1)}, bf16[64,2048]{1,0:T(8,128)(2,1)S(1)}, u32[]{:S(2)}, u32[]{:S(2)}) collective-permute-start(bf16[64,2048]{1,0:T(8,128)(2,1)S(1)} %get-tuple-element.36.refs_0_), channel_id=1, source_target_pairs={{0,4},{12,8},{1,5},{13,9},{2,6},{14,10},{3,7},{15,11},{16,20},{28,... | collective-permute-start | bytes 786440 | tf_op jit(solution)/shard_map/ppermute | solution.py:343
  19.9 5.1 %collective-permute-start.6 = (bf16[64,2048]{1,0:T(8,128)(2,1)S(1)}, bf16[64,2048]{1,0:T(8,128)(2,1)S(1)}, u32[]{:S(2)}, u32[]{:S(2)}) collective-permute-start(bf16[64,2048]{1,0:T(8,128)(2,1)S(1)} %shard_map.76.refs_2_), channel_id=1, source_target_pairs={{4,8},{8,4},{5,9},{9,5},{6,10},{10,6},{7,11},{11,7},{20,24},{24,20... | collective-permute-start | bytes 786440 | tf_op jit(solution)/shard_map/ppermute | solution.py:351
  20.5 42.0 %copy-start.4 = (f32[1,2048]{1,0:T(1,128)S(1)}, f32[1,2048]{1,0:T(1,128)}, u32[]{:S(2)}) copy-start(f32[1,2048]{1,0:T(1,128)} %refs_2_.7) | copy-start | bytes 24580
  24.3 9.1 %collective-permute-start.4 = (bf16[64,2048]{1,0:T(8,128)(2,1)S(1)}, bf16[64,2048]{1,0:T(8,128)(2,1)S(1)}, u32[]{:S(2)}, u32[]{:S(2)}) collective-permute-start(bf16[64,2048]{1,0:T(8,128)(2,1)S(1)} %shard_map.77.refs_3_), channel_id=1, source_target_pairs={{4,8},{8,4},{5,9},{9,5},{6,10},{10,6},{7,11},{11,7},{20,24},{24,20... | collective-permute-start | bytes 786440 | tf_op jit(solution)/shard_map/ppermute | solution.py:351
  25.0 37.6 %copy-start.2 = (bf16[1,1,768,2048]{3,2,1,0:T(8,128)(2,1)S(1)}, bf16[1,1,768,2048]{3,2,1,0:T(8,128)(2,1)}, u32[]{:S(2)}) copy-start(bf16[1,1,768,2048]{3,2,1,0:T(8,128)(2,1)} %param.13) | copy-start | bytes 9437188
  25.0 12.1 %collective-permute-start = (bf16[64,2048]{1,0:T(8,128)(2,1)S(1)}, bf16[64,2048]{1,0:T(8,128)(2,1)S(1)}, u32[]{:S(2)}, u32[]{:S(2)}) collective-permute-start(bf16[64,2048]{1,0:T(8,128)(2,1)S(1)} %get-tuple-element.33.refs_0_), channel_id=1, source_target_pairs={{0,4},{12,8},{1,5},{13,9},{2,6},{14,10},{3,7},{15,11},{16,20},{28,... | collective-permute-start | bytes 786440 | tf_op jit(solution)/shard_map/ppermute | solution.py:343
  33.4 9.1 %collective-permute-start.10 = (bf16[64,2048]{1,0:T(8,128)(2,1)S(1)}, bf16[64,2048]{1,0:T(8,128)(2,1)S(1)}, u32[]{:S(2)}, u32[]{:S(2)}) collective-permute-start(bf16[64,2048]{1,0:T(8,128)(2,1)S(1)} %shard_map.78.refs_2_.refs_0_), channel_id=1, source_target_pairs={{4,0},{8,12},{5,1},{9,13},{6,2},{10,14},{7,3},{11,15},{20,16},{24,... | collective-permute-start | bytes 786440 | tf_op jit(solution)/shard_map/ppermute | solution.py:359
  34.7 27.8 %copy-start.1 = (bf16[1,1,2048,768]{3,2,1,0:T(8,128)(2,1)S(1)}, bf16[1,1,2048,768]{3,2,1,0:T(8,128)(2,1)}, u32[]{:S(2)}) copy-start(bf16[1,1,2048,768]{3,2,1,0:T(8,128)(2,1)} %param.12) | copy-start | bytes 9437188
  34.9 27.7 %copy-start = (bf16[1,1,2048,768]{3,2,1,0:T(8,128)(2,1)S(1)}, bf16[1,1,2048,768]{3,2,1,0:T(8,128)(2,1)}, u32[]{:S(2)}) copy-start(bf16[1,1,2048,768]{3,2,1,0:T(8,128)(2,1)} %param.11) | copy-start | bytes 9437188
  37.2 6.0 %collective-permute-start.7 = (bf16[64,2048]{1,0:T(8,128)(2,1)S(1)}, bf16[64,2048]{1,0:T(8,128)(2,1)S(1)}, u32[]{:S(2)}, u32[]{:S(2)}) collective-permute-start(bf16[64,2048]{1,0:T(8,128)(2,1)S(1)} %shard_map.81.refs_2_), channel_id=1, source_target_pairs={{4,8},{8,4},{5,9},{9,5},{6,10},{10,6},{7,11},{11,7},{20,24},{24,20... | collective-permute-start | bytes 786440 | tf_op jit(solution)/shard_map/ppermute | solution.py:351
  42.5 2.0 %collective-permute-start.9 = (bf16[64,2048]{1,0:T(8,128)(2,1)S(1)}, bf16[64,2048]{1,0:T(8,128)(2,1)S(1)}, u32[]{:S(2)}, u32[]{:S(2)}) collective-permute-start(bf16[64,2048]{1,0:T(8,128)(2,1)S(1)} %shard_map.79.refs_3_), channel_id=1, source_target_pairs={{4,8},{8,4},{5,9},{9,5},{6,10},{10,6},{7,11},{11,7},{20,24},{24,20... | collective-permute-start | bytes 786440 | tf_op jit(solution)/shard_map/ppermute | solution.py:351
  43.2 14.9 %collective-permute-start.8 = (bf16[64,2048]{1,0:T(8,128)(2,1)S(1)}, bf16[64,2048]{1,0:T(8,128)(2,1)S(1)}, u32[]{:S(2)}, u32[]{:S(2)}) collective-permute-start(bf16[64,2048]{1,0:T(8,128)(2,1)S(1)} %shard_map.80.refs_2_.refs_0_), channel_id=1, source_target_pairs={{4,0},{8,12},{5,1},{9,13},{6,2},{10,14},{7,3},{11,15},{20,16},{24,... | collective-permute-start | bytes 786440 | tf_op jit(solution)/shard_map/ppermute | solution.py:359
  44.5 15.0 %collective-permute-start.13 = (bf16[64,2048]{1,0:T(8,128)(2,1)S(1)}, bf16[64,2048]{1,0:T(8,128)(2,1)S(1)}, u32[]{:S(2)}, u32[]{:S(2)}) collective-permute-start(bf16[64,2048]{1,0:T(8,128)(2,1)S(1)} %shard_map.82.refs_3_.refs_0_.refs_2_), channel_id=1, source_target_pairs={{0,2},{1,3},{2,0},{3,1},{4,6},{5,7},{6,4},{7,5},{8,10},{9,11},{10,... | collective-permute-start | bytes 786440 | tf_op jit(solution)/shard_map/ppermute | solution.py:323
  58.0 10.2 %collective-permute-start.12 = (bf16[64,2048]{1,0:T(8,128)(2,1)S(1)}, bf16[64,2048]{1,0:T(8,128)(2,1)S(1)}, u32[]{:S(2)}, u32[]{:S(2)}) collective-permute-start(bf16[64,2048]{1,0:T(8,128)(2,1)S(1)} %shard_map.83.refs_2_.refs_0_), channel_id=1, source_target_pairs={{4,0},{8,12},{5,1},{9,13},{6,2},{10,14},{7,3},{11,15},{20,16},{24,... | collective-permute-start | bytes 786440 | tf_op jit(solution)/shard_map/ppermute | solution.py:359
  59.5 12.1 %collective-permute-start.11 = (bf16[64,2048]{1,0:T(8,128)(2,1)S(1)}, bf16[64,2048]{1,0:T(8,128)(2,1)S(1)}, u32[]{:S(2)}, u32[]{:S(2)}) collective-permute-start(bf16[64,2048]{1,0:T(8,128)(2,1)S(1)} %shard_map.85.refs_10_.refs_0_), channel_id=1, source_target_pairs={{4,0},{8,12},{5,1},{9,13},{6,2},{10,14},{7,3},{11,15},{20,16},{24,... | collective-permute-start | bytes 786440 | tf_op jit(solution)/shard_map/ppermute | solution.py:359
  61.0 13.0 %collective-permute-start.20 = (bf16[64,2048]{1,0:T(8,128)(2,1)S(1)}, bf16[64,2048]{1,0:T(8,128)(2,1)S(1)}, u32[]{:S(2)}, u32[]{:S(2)}) collective-permute-start(bf16[64,2048]{1,0:T(8,128)(2,1)S(1)} %shard_map.84.refs_3_.refs_0_.refs_2_), channel_id=1, source_target_pairs={{0,2},{1,3},{2,0},{3,1},{4,6},{5,7},{6,4},{7,5},{8,10},{9,11},{10,... | collective-permute-start | bytes 786440 | tf_op jit(solution)/shard_map/ppermute | solution.py:323
  65.5 11.5 %collective-permute-start.19 = (bf16[128,1024]{1,0:T(8,128)(2,1)S(1)}, bf16[128,1024]{1,0:T(8,128)(2,1)S(1)}, u32[]{:S(2)}, u32[]{:S(2)}) collective-permute-start(bf16[128,1024]{1,0:T(8,128)(2,1)S(1)} %get-tuple-element.37.refs_2_), channel_id=1, source_target_pairs={{0,4},{4,0},{8,12},{12,8},{1,5},{5,1},{9,13},{13,9},{2,6},{6,2},{1... | collective-permute-start | bytes 786440 | tf_op jit(solution)/shard_map/ppermute | solution.py:323
  68.3 8.8 %collective-permute-start.18 = (bf16[64,2048]{1,0:T(8,128)(2,1)S(1)}, bf16[64,2048]{1,0:T(8,128)(2,1)S(1)}, u32[]{:S(2)}, u32[]{:S(2)}) collective-permute-start(bf16[64,2048]{1,0:T(8,128)(2,1)S(1)} %shard_map.87.refs_2_.refs_0_), channel_id=1, source_target_pairs={{0,2},{1,3},{2,0},{3,1},{4,6},{5,7},{6,4},{7,5},{8,10},{9,11},{10,... | collective-permute-start | bytes 786440 | tf_op jit(solution)/shard_map/ppermute | solution.py:323
  71.6 10.9 %collective-permute-start.17 = (bf16[64,2048]{1,0:T(8,128)(2,1)S(1)}, bf16[64,2048]{1,0:T(8,128)(2,1)S(1)}, u32[]{:S(2)}, u32[]{:S(2)}) collective-permute-start(bf16[64,2048]{1,0:T(8,128)(2,1)S(1)} %shard_map.88.refs_10_.refs_0_.refs_2_), channel_id=1, source_target_pairs={{0,2},{1,3},{2,0},{3,1},{4,6},{5,7},{6,4},{7,5},{8,10},{9,11},{10,... | collective-permute-start | bytes 786440 | tf_op jit(solution)/shard_map/ppermute | solution.py:323
  76.9 11.2 %collective-permute-start.24 = (bf16[128,1024]{1,0:T(8,128)(2,1)S(1)}, bf16[128,1024]{1,0:T(8,128)(2,1)S(1)}, u32[]{:S(2)}, u32[]{:S(2)}) collective-permute-start(bf16[128,1024]{1,0:T(8,128)(2,1)S(1)} %get-tuple-element.39.refs_2_), channel_id=1, source_target_pairs={{0,4},{4,0},{8,12},{12,8},{1,5},{5,1},{9,13},{13,9},{2,6},{6,2},{1... | collective-permute-start | bytes 786440 | tf_op jit(solution)/shard_map/ppermute | solution.py:323
  80.0 17.2 %collective-permute-start.22 = (bf16[64,2048]{1,0:T(8,128)(2,1)S(1)}, bf16[64,2048]{1,0:T(8,128)(2,1)S(1)}, u32[]{:S(2)}, u32[]{:S(2)}) collective-permute-start(bf16[64,2048]{1,0:T(8,128)(2,1)S(1)} %get-tuple-element.41.refs_10_), channel_id=1, source_target_pairs={{0,2},{1,3},{2,0},{3,1},{4,6},{5,7},{6,4},{7,5},{8,10},{9,11},{10,... | collective-permute-start | bytes 786440 | tf_op jit(solution)/shard_map/ppermute | solution.py:323
  85.4 12.0 %collective-permute-start.21 = (bf16[64,2048]{1,0:T(8,128)(2,1)S(1)}, bf16[64,2048]{1,0:T(8,128)(2,1)S(1)}, u32[]{:S(2)}, u32[]{:S(2)}) collective-permute-start(bf16[64,2048]{1,0:T(8,128)(2,1)S(1)} %get-tuple-element.43.refs_2_), channel_id=1, source_target_pairs={{0,2},{1,3},{2,0},{3,1},{4,6},{5,7},{6,4},{7,5},{8,10},{9,11},{10,... | collective-permute-start | bytes 786440 | tf_op jit(solution)/shard_map/ppermute | solution.py:323
  86.2 11.0 %collective-permute-start.23 = (bf16[128,512]{1,0:T(8,128)(2,1)S(1)}, bf16[128,512]{1,0:T(8,128)(2,1)S(1)}, u32[]{:S(2)}, u32[]{:S(2)}) collective-permute-start(bf16[128,512]{1,0:T(8,128)(2,1)S(1)} %get-tuple-element.40.refs_10_), channel_id=1, source_target_pairs={{0,8},{4,12},{8,0},{12,4},{1,9},{5,13},{9,1},{13,5},{2,10},{6,14},... | collective-permute-start | bytes 393224 | tf_op jit(solution)/shard_map/ppermute | solution.py:323
  88.1 11.6 %collective-permute-start.28 = (bf16[128,512]{1,0:T(8,128)(2,1)S(1)}, bf16[128,512]{1,0:T(8,128)(2,1)S(1)}, u32[]{:S(2)}, u32[]{:S(2)}) collective-permute-start(bf16[128,512]{1,0:T(8,128)(2,1)S(1)} %get-tuple-element.47.refs_2_), channel_id=1, source_target_pairs={{0,8},{4,12},{8,0},{12,4},{1,9},{5,13},{9,1},{13,5},{2,10},{6,14},... | collective-permute-start | bytes 393224 | tf_op jit(solution)/shard_map/ppermute | solution.py:323
  97.3 5.0 %collective-permute-start.27 = (bf16[64,1024]{1,0:T(8,128)(2,1)S(1)}, bf16[64,1024]{1,0:T(8,128)(2,1)S(1)}, u32[]{:S(2)}, u32[]{:S(2)}) collective-permute-start(bf16[64,1024]{1,0:T(8,128)(2,1)S(1)} %get-tuple-element.49.refs_2_), channel_id=1, source_target_pairs={{0,4},{4,0},{8,12},{12,8},{1,5},{5,1},{9,13},{13,9},{2,6},{6,2},{1... | collective-permute-start | bytes 393224 | tf_op jit(solution)/shard_map/ppermute | solution.py:323
  97.5 6.4 %collective-permute-start.25 = (bf16[64,1024]{1,0:T(8,128)(2,1)S(1)}, bf16[64,1024]{1,0:T(8,128)(2,1)S(1)}, u32[]{:S(2)}, u32[]{:S(2)}) collective-permute-start(bf16[64,1024]{1,0:T(8,128)(2,1)S(1)} %get-tuple-element.51.refs_2_), channel_id=1, source_target_pairs={{0,4},{4,0},{8,12},{12,8},{1,5},{5,1},{9,13},{13,9},{2,6},{6,2},{1... | collective-permute-start | bytes 393224 | tf_op jit(solution)/shard_map/ppermute | solution.py:323
  99.5 4.3 %collective-permute-start.26 = (bf16[64,512]{1,0:T(8,128)(2,1)S(1)}, bf16[64,512]{1,0:T(8,128)(2,1)S(1)}, u32[]{:S(2)}, u32[]{:S(2)}) collective-permute-start(bf16[64,512]{1,0:T(8,128)(2,1)S(1)} %get-tuple-element.48.refs_2_), channel_id=1, source_target_pairs={{0,2},{1,3},{2,0},{3,1},{4,6},{5,7},{6,4},{7,5},{8,10},{9,11},{10,... | collective-permute-start | bytes 196616 | tf_op jit(solution)/shard_map/ppermute | solution.py:323
  99.7 5.8 %collective-permute-start.30 = (bf16[64,512]{1,0:T(8,128)(2,1)S(1)}, bf16[64,512]{1,0:T(8,128)(2,1)S(1)}, u32[]{:S(2)}, u32[]{:S(2)}) collective-permute-start(bf16[64,512]{1,0:T(8,128)(2,1)S(1)} %get-tuple-element.55.refs_2_), channel_id=1, source_target_pairs={{0,2},{1,3},{2,0},{3,1},{4,6},{5,7},{6,4},{7,5},{8,10},{9,11},{10,... | collective-permute-start | bytes 196616 | tf_op jit(solution)/shard_map/ppermute | solution.py:323
  102.4 5.4 %collective-permute-start.31 = (bf16[64,512]{1,0:T(8,128)(2,1)S(1)}, bf16[64,512]{1,0:T(8,128)(2,1)S(1)}, u32[]{:S(2)}, u32[]{:S(2)}) collective-permute-start(bf16[64,512]{1,0:T(8,128)(2,1)S(1)} %get-tuple-element.56.refs_3_), channel_id=1, source_target_pairs={{0,8},{4,12},{8,0},{12,4},{1,9},{5,13},{9,1},{13,5},{2,10},{6,14},... | collective-permute-start | bytes 196616 | tf_op jit(solution)/shard_map/ppermute | solution.py:323
  103.9 5.2 %collective-permute-start.29 = (bf16[64,512]{1,0:T(8,128)(2,1)S(1)}, bf16[64,512]{1,0:T(8,128)(2,1)S(1)}, u32[]{:S(2)}, u32[]{:S(2)}) collective-permute-start(bf16[64,512]{1,0:T(8,128)(2,1)S(1)} %get-tuple-element.58.refs_3_), channel_id=1, source_target_pairs={{0,8},{4,12},{8,0},{12,4},{1,9},{5,13},{9,1},{13,5},{2,10},{6,14},... | collective-permute-start | bytes 196616 | tf_op jit(solution)/shard_map/ppermute | solution.py:323

commit v2 on v1

--- a/solution.py
+++ b/solution.py
@@ -10,7 +10,7 @@
 CHUNKS = (1, 1, 1, 1)
 HOP, START, MIDDLE, WIRE, EXPERT = 2.5, 2.0, 0.0, 22.5, 16.0
 SLACK, OLDEST = 0.0, False
-TUNED = ()
+TUNED = ((0, 0), (1, 0), (0, 1), (2, 0), (1, 1), (0, 2), (3, 0), (2, 1), (1, 2), (3, 1), (0, 3), (2, 2), (3, 2), (1, 3), (0, 4), (2, 3), (3, 3), (1, 4), (0, 5), (2, 4), (3, 4), (1, 5), (2, 5), (0, 6), (3, 5), (1, 6), (2, 6), (3, 6))
 ROWS_FIRST = 2
 
 
@@ -301,10 +301,10 @@
     starts = [sum(sizes[:c]) for c in range(len(sizes))]
     to_vmem = lambda value: pltpu.with_memory_space_constraint(value, pltpu.VMEM)
 
-    weights = [
-        (to_vmem(value[0, 0]), to_vmem(swap(value[0, 0], "expert", near)))
-        for value in (w_gate, w_up, w_down)
-    ]
+    weights = []
+    for value in (w_gate, w_up, w_down):
+        other = swap(value[0, 0], "expert", near)
+        weights.append((to_vmem(value[0, 0]), to_vmem(other)))
     turned = [jnp.swapaxes(value, 1, 2)[0] for value in (routes, route_gates)]
     tables = list(call(table_body, [full_of(experts, tok_rows)], turned))
     for bit in far_bits:

time: 110 us -> 107 us (0.973)
  waiting for transfers between devices: 44 us -> 34.8 us
  starting transfers between devices: 48.9 us -> 55.3 us
    ppermute x16, starting transfers between devices: 19.9 us -> 26.4 us  [trade(): lax.ppermute(value, axis, [(i, i ^ bit) for i in range(lax.axis_size(axis...]
    ppermute x4, waiting for transfers between devices: 19.2 us -> 12.8 us  [spread(): st['came'] = lax.ppermute(st['total'], 'track', outward(step))]
    ppermute x16, waiting for transfers between devices: 14.7 us -> 11.9 us  [trade(): lax.ppermute(value, axis, [(i, i ^ bit) for i in range(lax.axis_size(axis...]
  transfers between devices with their start and end apart: 32 -> 32, of which waited for: 13 -> 12; matrix products, arithmetic and copies ran while one was open for 0% -> 0% of each run, Pallas kernels for 12% -> 12%
where the time goes in v2:
time: 107 us
  starting transfers between devices  55.3 us (52%)
  waiting for transfers between devices  34.8 us (33%)
  Pallas kernels  13.9 us (13%)
  local copies, waits for them, and re-layouts  2.61 us (2%)
    ppermute x16, starting transfers between devices, trade(): lax.ppermute(value, axis, [(i, i ^ bit) for i in range(lax.axis_size(axis...  26.4 us
    ppermute x4, starting transfers between devices, begin(): lax.ppermute(own, 'track', inward(0) if middle > 1 else across)  18.4 us
    pallas_call x31, Pallas kernels, call(): pl.pallas_call(kernel, out_shape=outs, in_specs=[space] * len(ins) + [ANY...  13.9 us
    ppermute x4, waiting for transfers between devices, spread(): st['came'] = lax.ppermute(st['total'], 'track', outward(step))  12.8 us
    ppermute x16, waiting for transfers between devices, trade(): lax.ppermute(value, axis, [(i, i ^ bit) for i in range(lax.axis_size(axis...  11.9 us
    ppermute x4, waiting for transfers between devices, begin(): lax.ppermute(own, 'track', inward(0) if middle > 1 else across)  7.98 us
    ppermute x4, starting transfers between devices, spread(): st['came'] = lax.ppermute(st['total'], 'track', outward(step))  5.33 us
    ppermute x4, starting transfers between devices, gather(): st['came'] = lax.ppermute(total, 'track', link)  2.66 us
  transfers between devices with their start and end apart: 32, of which 12 were waited for; matrix products, arithmetic and copies ran while one was open for 0% of the time, Pallas kernels for 12%

profile of v2, /device:TPU:0, one launch (start us, length us, event | category | flops | bytes accessed | tf_op | source)
XLA Modules:
  0.0 107.0 jit_solution(9639284965065393671)
XLA Ops:
  0.0 0.5 collective-permute-start.14
  0.5 0.5 collective-permute-start.16
  1.0 1.2 %copy-done.3 = bf16[1,256,2048]{2,1,0:T(8,128)(2,1)S(1)} copy-done((bf16[1,256,2048]{2,1,0:T(8,128)(2,1)S(1)}, bf16[1,256,2048]{2,1,0:T(8,128)(2,1)}, u32[]{:S(2)}) %copy-start.3) | copy-done | bytes 1048600
  2.2 0.1 shard_map.73
  2.4 4.5 %collective-permute-start.1 = (bf16[64,2048]{1,0:T(8,128)(2,1)S(1)}, bf16[64,2048]{1,0:T(8,128)(2,1)S(1)}, u32[]{:S(2)}, u32[]{:S(2)}) collective-permute-start(bf16[64,2048]{1,0:T(8,128)(2,1)S(1)} %get-tuple-element.34.refs_0_), channel_id=1, source_target_pairs={{0,4},{12,8},{1,5},{13,9},{2,6},{14,10},{3,7},{15,11},{16,20},{28,... | collective-permute-start | bytes 786440 | tf_op jit(solution)/shard_map/ppermute | solution.py:343
  6.9 0.7 copy-done.5
  7.5 0.7 copy-done.6
  8.2 1.6 %collective-permute-start.2 = (f32[4,256]{1,0:T(4,128)S(1)}, f32[4,256]{1,0:T(4,128)S(1)}, u32[]{:S(2)}, u32[]{:S(2)}) collective-permute-start(f32[4,256]{1,0:T(4,128)S(1)} %shard_map.74.refs_0_), channel_id=1, source_target_pairs={{0,2},{1,3},{2,0},{3,1},{4,6},{5,7},{6,4},{7,5},{8,10},{9,11},{10,... | collective-permute-start | bytes 12296 | tf_op jit(solution)/shard_map/ppermute | solution.py:81
  9.8 2.1 %collective-permute-done.2.refs_1_ = f32[4,256]{1,0:T(4,128)S(1)} collective-permute-done((f32[4,256]{1,0:T(4,128)S(1)}, f32[4,256]{1,0:T(4,128)S(1)}, u32[]{:S(2)}, u32[]{:S(2)}) %collective-permute-start.2) | collective-permute-done | bytes 4128 | tf_op jit(solution)/shard_map/ppermute | solution.py:81
  11.9 1.3 %collective-permute-start.4 = (bf16[64,2048]{1,0:T(8,128)(2,1)S(1)}, bf16[64,2048]{1,0:T(8,128)(2,1)S(1)}, u32[]{:S(2)}, u32[]{:S(2)}) collective-permute-start(bf16[64,2048]{1,0:T(8,128)(2,1)S(1)} %get-tuple-element.35.refs_0_), channel_id=1, source_target_pairs={{0,4},{12,8},{1,5},{13,9},{2,6},{14,10},{3,7},{15,11},{16,20},{28,... | collective-permute-start | bytes 786440 | tf_op jit(solution)/shard_map/ppermute | solution.py:343
  13.2 4.3 %collective-permute-start.7 = (bf16[64,2048]{1,0:T(8,128)(2,1)S(1)}, bf16[64,2048]{1,0:T(8,128)(2,1)S(1)}, u32[]{:S(2)}, u32[]{:S(2)}) collective-permute-start(bf16[64,2048]{1,0:T(8,128)(2,1)S(1)} %get-tuple-element.36.refs_0_), channel_id=1, source_target_pairs={{0,4},{12,8},{1,5},{13,9},{2,6},{14,10},{3,7},{15,11},{16,20},{28,... | collective-permute-start | bytes 786440 | tf_op jit(solution)/shard_map/ppermute | solution.py:343
  17.6 0.1 shard_map.75.refs_2_.refs_3_
  17.7 0.1 shard_map.76.refs_2_
  17.8 2.1 %collective-permute-done.4.refs_1_ = bf16[64,2048]{1,0:T(8,128)(2,1)S(1)} collective-permute-done((bf16[64,2048]{1,0:T(8,128)(2,1)S(1)}, bf16[64,2048]{1,0:T(8,128)(2,1)S(1)}, u32[]{:S(2)}, u32[]{:S(2)}) %collective-permute-start.4) | collective-permute-done | bytes 262176 | tf_op jit(solution)/shard_map/ppermute | solution.py:343
  19.9 0.7 collective-permute-start.3
  20.6 0.1 shard_map.77.refs_3_
  20.6 3.7 %collective-permute-done.7.refs_1_ = bf16[64,2048]{1,0:T(8,128)(2,1)S(1)} collective-permute-done((bf16[64,2048]{1,0:T(8,128)(2,1)S(1)}, bf16[64,2048]{1,0:T(8,128)(2,1)S(1)}, u32[]{:S(2)}, u32[]{:S(2)}) %collective-permute-start.7) | collective-permute-done | bytes 262176 | tf_op jit(solution)/shard_map/ppermute | solution.py:343
  24.3 0.7 collective-permute-start.6
  25.0 8.3 %collective-permute-start = (bf16[64,2048]{1,0:T(8,128)(2,1)S(1)}, bf16[64,2048]{1,0:T(8,128)(2,1)S(1)}, u32[]{:S(2)}, u32[]{:S(2)}) collective-permute-start(bf16[64,2048]{1,0:T(8,128)(2,1)S(1)} %get-tuple-element.33.refs_0_), channel_id=1, source_target_pairs={{0,4},{12,8},{1,5},{13,9},{2,6},{14,10},{3,7},{15,11},{16,20},{28,... | collective-permute-start | bytes 786440 | tf_op jit(solution)/shard_map/ppermute | solution.py:343
  33.2 0.1 shard_map.78.refs_2_.refs_0_
  33.4 1.3 %collective-permute-start.5 = (bf16[64,2048]{1,0:T(8,128)(2,1)S(1)}, bf16[64,2048]{1,0:T(8,128)(2,1)S(1)}, u32[]{:S(2)}, u32[]{:S(2)}) collective-permute-start(bf16[64,2048]{1,0:T(8,128)(2,1)S(1)} %shard_map.78.refs_2_.refs_0_), channel_id=1, source_target_pairs={{4,0},{8,12},{5,1},{9,13},{6,2},{10,14},{7,3},{11,15},{20,16},{24,... | collective-permute-start | bytes 786440 | tf_op jit(solution)/shard_map/ppermute | solution.py:359
  34.7 0.1 shard_map.79.refs_3_
  34.7 0.1 shard_map.80.refs_2_.refs_0_
  34.9 2.2 %collective-permute-done.refs_1_ = bf16[64,2048]{1,0:T(8,128)(2,1)S(1)} collective-permute-done((bf16[64,2048]{1,0:T(8,128)(2,1)S(1)}, bf16[64,2048]{1,0:T(8,128)(2,1)S(1)}, u32[]{:S(2)}, u32[]{:S(2)}) %collective-permute-start) | collective-permute-done | bytes 262176 | tf_op jit(solution)/shard_map/ppermute | solution.py:343
  37.1 1.3 %collective-permute-start.9 = (bf16[64,2048]{1,0:T(8,128)(2,1)S(1)}, bf16[64,2048]{1,0:T(8,128)(2,1)S(1)}, u32[]{:S(2)}, u32[]{:S(2)}) collective-permute-start(bf16[64,2048]{1,0:T(8,128)(2,1)S(1)} %shard_map.80.refs_2_.refs_0_), channel_id=1, source_target_pairs={{4,0},{8,12},{5,1},{9,13},{6,2},{10,14},{7,3},{11,15},{20,16},{24,... | collective-permute-start | bytes 786440 | tf_op jit(solution)/shard_map/ppermute | solution.py:359
  38.4 6.2 %collective-permute-done.5.refs_1_ = bf16[64,2048]{1,0:T(8,128)(2,1)S(1)} collective-permute-done((bf16[64,2048]{1,0:T(8,128)(2,1)S(1)}, bf16[64,2048]{1,0:T(8,128)(2,1)S(1)}, u32[]{:S(2)}, u32[]{:S(2)}) %collective-permute-start.5) | collective-permute-done | bytes 262176 | tf_op jit(solution)/shard_map/ppermute | solution.py:359
  44.6 0.7 collective-permute-start.10
  45.4 0.1 shard_map.82.refs_3_
  45.4 2.7 %collective-permute-done.9.refs_1_ = bf16[64,2048]{1,0:T(8,128)(2,1)S(1)} collective-permute-done((bf16[64,2048]{1,0:T(8,128)(2,1)S(1)}, bf16[64,2048]{1,0:T(8,128)(2,1)S(1)}, u32[]{:S(2)}, u32[]{:S(2)}) %collective-permute-start.9) | collective-permute-done | bytes 262176 | tf_op jit(solution)/shard_map/ppermute | solution.py:359
  48.1 0.7 collective-permute-start.8
  48.8 1.6 %collective-permute-start.13 = (bf16[64,2048]{1,0:T(8,128)(2,1)S(1)}, bf16[64,2048]{1,0:T(8,128)(2,1)S(1)}, u32[]{:S(2)}, u32[]{:S(2)}) collective-permute-start(bf16[64,2048]{1,0:T(8,128)(2,1)S(1)} %shard_map.81.refs_2_.refs_0_), channel_id=1, source_target_pairs={{0,2},{1,3},{2,0},{3,1},{4,6},{5,7},{6,4},{7,5},{8,10},{9,11},{10,... | collective-permute-start | bytes 786440 | tf_op jit(solution)/shard_map/ppermute | solution.py:323
  50.3 0.1 shard_map.83.refs_2_.refs_0_
  50.4 1.3 %collective-permute-start.12 = (bf16[64,2048]{1,0:T(8,128)(2,1)S(1)}, bf16[64,2048]{1,0:T(8,128)(2,1)S(1)}, u32[]{:S(2)}, u32[]{:S(2)}) collective-permute-start(bf16[64,2048]{1,0:T(8,128)(2,1)S(1)} %shard_map.83.refs_2_.refs_0_), channel_id=1, source_target_pairs={{4,0},{8,12},{5,1},{9,13},{6,2},{10,14},{7,3},{11,15},{20,16},{24,... | collective-permute-start | bytes 786440 | tf_op jit(solution)/shard_map/ppermute | solution.py:359
  51.8 0.1 shard_map.85.refs_10_.refs_0_
  51.9 3.3 %collective-permute-done.13.refs_1_ = bf16[64,2048]{1,0:T(8,128)(2,1)S(1)} collective-permute-done((bf16[64,2048]{1,0:T(8,128)(2,1)S(1)}, bf16[64,2048]{1,0:T(8,128)(2,1)S(1)}, u32[]{:S(2)}, u32[]{:S(2)}) %collective-permute-start.13) | collective-permute-done | bytes 262176 | tf_op jit(solution)/shard_map/ppermute | solution.py:323
  55.2 1.5 %collective-permute-start.11 = (bf16[64,2048]{1,0:T(8,128)(2,1)S(1)}, bf16[64,2048]{1,0:T(8,128)(2,1)S(1)}, u32[]{:S(2)}, u32[]{:S(2)}) collective-permute-start(bf16[64,2048]{1,0:T(8,128)(2,1)S(1)} %shard_map.85.refs_10_.refs_0_), channel_id=1, source_target_pairs={{4,0},{8,12},{5,1},{9,13},{6,2},{10,14},{7,3},{11,15},{20,16},{24,... | collective-permute-start | bytes 786440 | tf_op jit(solution)/shard_map/ppermute | solution.py:359
  56.7 1.6 %collective-permute-start.20 = (bf16[64,2048]{1,0:T(8,128)(2,1)S(1)}, bf16[64,2048]{1,0:T(8,128)(2,1)S(1)}, u32[]{:S(2)}, u32[]{:S(2)}) collective-permute-start(bf16[64,2048]{1,0:T(8,128)(2,1)S(1)} %shard_map.84.refs_3_.refs_0_.refs_2_), channel_id=1, source_target_pairs={{0,2},{1,3},{2,0},{3,1},{4,6},{5,7},{6,4},{7,5},{8,10},{9,11},{10,... | collective-permute-start | bytes 786440 | tf_op jit(solution)/shard_map/ppermute | solution.py:323
  58.3 2.9 %shard_map.86 = (f32[128,1024]{1,0:T(8,128)S(1)}, bf16[128,1024]{1,0:T(8,128)(2,1)S(1)}) custom-call(bf16[64,2048]{1,0:T(8,128)(2,1)S(1)} %shard_map.81.refs_2_.refs_0_, bf16[64,2048]{1,0:T(8,128)(2,1)S(1)} %collective-permute-done.13.refs_1_, f32[1,2048]{1,0:T(1,128)S(1)} %copy-done.4, f32[2,256,8]{2,1,0:T(8,128)S(1)} %shard_map.75.refs_2_.refs_3_, ...), custom_call_target="tpu_custom_call" | custom-call | tf_op jit(solution)/shard_map/pallas_call | solution.py:102
  61.2 6.1 %collective-permute-start.19 = (bf16[128,1024]{1,0:T(8,128)(2,1)S(1)}, bf16[128,1024]{1,0:T(8,128)(2,1)S(1)}, u32[]{:S(2)}, u32[]{:S(2)}) collective-permute-start(bf16[128,1024]{1,0:T(8,128)(2,1)S(1)} %get-tuple-element.37.refs_2_), channel_id=1, source_target_pairs={{0,4},{4,0},{8,12},{12,8},{1,5},{5,1},{9,13},{13,9},{2,6},{6,2},{1... | collective-permute-start | bytes 786440 | tf_op jit(solution)/shard_map/ppermute | solution.py:323
  67.3 0.7 collective-permute-start.18
  68.1 3.9 %collective-permute-done.11.refs_1_ = bf16[64,2048]{1,0:T(8,128)(2,1)S(1)} collective-permute-done((bf16[64,2048]{1,0:T(8,128)(2,1)S(1)}, bf16[64,2048]{1,0:T(8,128)(2,1)S(1)}, u32[]{:S(2)}, u32[]{:S(2)}) %collective-permute-start.11) | collective-permute-done | bytes 262176 | tf_op jit(solution)/shard_map/ppermute | solution.py:359
  72.0 1.6 %collective-permute-start.17 = (bf16[64,2048]{1,0:T(8,128)(2,1)S(1)}, bf16[64,2048]{1,0:T(8,128)(2,1)S(1)}, u32[]{:S(2)}, u32[]{:S(2)}) collective-permute-start(bf16[64,2048]{1,0:T(8,128)(2,1)S(1)} %shard_map.88.refs_10_.refs_0_.refs_2_), channel_id=1, source_target_pairs={{0,2},{1,3},{2,0},{3,1},{4,6},{5,7},{6,4},{7,5},{8,10},{9,11},{10,... | collective-permute-start | bytes 786440 | tf_op jit(solution)/shard_map/ppermute | solution.py:323
  73.5 2.9 %shard_map.89 = (f32[128,1024]{1,0:T(8,128)S(1)}, bf16[128,1024]{1,0:T(8,128)(2,1)S(1)}) custom-call(bf16[64,2048]{1,0:T(8,128)(2,1)S(1)} %shard_map.84.refs_3_.refs_0_.refs_2_, bf16[64,2048]{1,0:T(8,128)(2,1)S(1)} %collective-permute-done.20.refs_1_, f32[1,2048]{1,0:T(1,128)S(1)} %copy-done.4, f32[2,256,8]{2,1,0:T(8,128)S(1)} %shard_map.75.refs_2_.refs_3_, ...), custom_call_target="tpu_custom_call" | custom-call | tf_op jit(solution)/shard_map/pallas_call | solution.py:102
  76.4 0.1 collective-permute-start.24
  76.5 0.1 shard_map.90
  76.6 2.9 %shard_map.91 = (f32[64,2048]{1,0:T(8,128)S(1)}, bf16[64,2048]{1,0:T(8,128)(2,1)S(1)}) custom-call(bf16[64,2048]{1,0:T(8,128)(2,1)S(1)} %shard_map.87.refs_2_.refs_0_, bf16[64,2048]{1,0:T(8,128)(2,1)S(1)} %collective-permute-done.18.refs_1_, f32[1,2048]{1,0:T(1,128)S(1)} %copy-done.4, f32[2,256,8]{2,1,0:T(8,128)S(1)} %shard_map.75.refs_2_.refs_3_, ...), custom_call_target="tpu_custom_call" | custom-call | tf_op jit(solution)/shard_map/pallas_call | solution.py:102
  79.5 2.3 %collective-permute-start.22 = (bf16[64,2048]{1,0:T(8,128)(2,1)S(1)}, bf16[64,2048]{1,0:T(8,128)(2,1)S(1)}, u32[]{:S(2)}, u32[]{:S(2)}) collective-permute-start(bf16[64,2048]{1,0:T(8,128)(2,1)S(1)} %get-tuple-element.41.refs_10_), channel_id=1, source_target_pairs={{0,2},{1,3},{2,0},{3,1},{4,6},{5,7},{6,4},{7,5},{8,10},{9,11},{10,... | collective-permute-start | bytes 786440 | tf_op jit(solution)/shard_map/ppermute | solution.py:323
  81.8 2.9 %shard_map.92 = (f32[64,2048]{1,0:T(8,128)S(1)}, bf16[64,2048]{1,0:T(8,128)(2,1)S(1)}) custom-call(bf16[64,2048]{1,0:T(8,128)(2,1)S(1)} %shard_map.88.refs_10_.refs_0_.refs_2_, bf16[64,2048]{1,0:T(8,128)(2,1)S(1)} %collective-permute-done.17.refs_1_, f32[1,2048]{1,0:T(1,128)S(1)} %copy-done.4, f32[2,256,8]{2,1,0:T(8,128)S(1)} %shard_map.75.refs_2_.refs_3_, ...), custom_call_target="tpu_custom_call" | custom-call | tf_op jit(solution)/shard_map/pallas_call | solution.py:102
  84.8 0.1 collective-permute-start.21
  84.8 2.8 %collective-permute-start.23 = (bf16[128,512]{1,0:T(8,128)(2,1)S(1)}, bf16[128,512]{1,0:T(8,128)(2,1)S(1)}, u32[]{:S(2)}, u32[]{:S(2)}) collective-permute-start(bf16[128,512]{1,0:T(8,128)(2,1)S(1)} %get-tuple-element.40.refs_10_), channel_id=1, source_target_pairs={{0,8},{4,12},{8,0},{12,4},{1,9},{5,13},{9,1},{13,5},{2,10},{6,14},... | collective-permute-start | bytes 393224 | tf_op jit(solution)/shard_map/ppermute | solution.py:323
  87.6 0.1 shard_map.93
  87.7 0.3 collective-permute-start.28
  87.9 3.5 %collective-permute-done.23.refs_1_ = bf16[128,512]{1,0:T(8,128)(2,1)S(1)} collective-permute-done((bf16[128,512]{1,0:T(8,128)(2,1)S(1)}, bf16[128,512]{1,0:T(8,128)(2,1)S(1)}, u32[]{:S(2)}, u32[]{:S(2)}) %collective-permute-start.23) | collective-permute-done | bytes 131104 | tf_op jit(solution)/shard_map/ppermute | solution.py:323
  91.5 0.1 shard_map.95
  91.6 2.5 %collective-permute-start.27 = (bf16[64,1024]{1,0:T(8,128)(2,1)S(1)}, bf16[64,1024]{1,0:T(8,128)(2,1)S(1)}, u32[]{:S(2)}, u32[]{:S(2)}) collective-permute-start(bf16[64,1024]{1,0:T(8,128)(2,1)S(1)} %get-tuple-element.49.refs_2_), channel_id=1, source_target_pairs={{0,4},{4,0},{8,12},{12,8},{1,5},{5,1},{9,13},{13,9},{2,6},{6,2},{1... | collective-permute-start | bytes 393224 | tf_op jit(solution)/shard_map/ppermute | solution.py:323
  94.1 0.1 collective-permute-start.25
  94.2 2.1 %collective-permute-start.26 = (bf16[64,512]{1,0:T(8,128)(2,1)S(1)}, bf16[64,512]{1,0:T(8,128)(2,1)S(1)}, u32[]{:S(2)}, u32[]{:S(2)}) collective-permute-start(bf16[64,512]{1,0:T(8,128)(2,1)S(1)} %get-tuple-element.48.refs_2_), channel_id=1, source_target_pairs={{0,2},{1,3},{2,0},{3,1},{4,6},{5,7},{6,4},{7,5},{8,10},{9,11},{10,... | collective-permute-start | bytes 196616 | tf_op jit(solution)/shard_map/ppermute | solution.py:323
  96.3 0.4 collective-permute-start.30
  96.7 1.0 collective-permute-done.27.refs_1_
  97.7 2.5 %collective-permute-start.31 = (bf16[64,512]{1,0:T(8,128)(2,1)S(1)}, bf16[64,512]{1,0:T(8,128)(2,1)S(1)}, u32[]{:S(2)}, u32[]{:S(2)}) collective-permute-start(bf16[64,512]{1,0:T(8,128)(2,1)S(1)} %get-tuple-element.56.refs_3_), channel_id=1, source_target_pairs={{0,8},{4,12},{8,0},{12,4},{1,9},{5,13},{9,1},{13,5},{2,10},{6,14},... | collective-permute-start | bytes 196616 | tf_op jit(solution)/shard_map/ppermute | solution.py:323
  100.3 1.9 %collective-permute-start.29 = (bf16[64,512]{1,0:T(8,128)(2,1)S(1)}, bf16[64,512]{1,0:T(8,128)(2,1)S(1)}, u32[]{:S(2)}, u32[]{:S(2)}) collective-permute-start(bf16[64,512]{1,0:T(8,128)(2,1)S(1)} %get-tuple-element.58.refs_3_), channel_id=1, source_target_pairs={{0,8},{4,12},{8,0},{12,4},{1,9},{5,13},{9,1},{13,5},{2,10},{6,14},... | collective-permute-start | bytes 196616 | tf_op jit(solution)/shard_map/ppermute | solution.py:323
  102.2 0.7 collective-permute-done.31.refs_1_
  103.0 3.3 %collective-permute-done.29.refs_1_ = bf16[64,512]{1,0:T(8,128)(2,1)S(1)} collective-permute-done((bf16[64,512]{1,0:T(8,128)(2,1)S(1)}, bf16[64,512]{1,0:T(8,128)(2,1)S(1)}, u32[]{:S(2)}, u32[]{:S(2)}) %collective-permute-start.29) | collective-permute-done | bytes 65568 | tf_op jit(solution)/shard_map/ppermute | solution.py:323
  106.3 0.7 shard_map.103
  (45 shorter events, 0.5 us)
Async XLA Ops:
  0.0 56.7 %collective-permute-start.14 = (bf16[2048,768]{1,0:T(8,128)(2,1)}, bf16[2048,768]{1,0:T(8,128)(2,1)S(1)}, u32[]{:S(2)}, u32[]{:S(2)}) collective-permute-start(bf16[2048,768]{1,0:T(8,128)(2,1)} %bitcast.10), channel_id=1, source_target_pairs={{0,1},{1,0},{2,3},{3,2},{4,5},{5,4},{6,7},{7,6},{8,9},{9,8},{10,11... | collective-permute-start | bytes 9437192 | tf_op jit(solution)/shard_map/ppermute | solution.py:81
  0.5 57.8 %collective-permute-start.15 = (bf16[2048,768]{1,0:T(8,128)(2,1)}, bf16[2048,768]{1,0:T(8,128)(2,1)S(1)}, u32[]{:S(2)}, u32[]{:S(2)}) collective-permute-start(bf16[2048,768]{1,0:T(8,128)(2,1)} %bitcast.15), channel_id=1, source_target_pairs={{0,1},{1,0},{2,3},{3,2},{4,5},{5,4},{6,7},{7,6},{8,9},{9,8},{10,11... | collective-permute-start | bytes 9437192 | tf_op jit(solution)/shard_map/ppermute | solution.py:81
  0.5 57.7 %collective-permute-start.16 = (bf16[768,2048]{1,0:T(8,128)(2,1)}, bf16[768,2048]{1,0:T(8,128)(2,1)S(1)}, u32[]{:S(2)}, u32[]{:S(2)}) collective-permute-start(bf16[768,2048]{1,0:T(8,128)(2,1)} %bitcast.20), channel_id=1, source_target_pairs={{0,1},{1,0},{2,3},{3,2},{4,5},{5,4},{6,7},{7,6},{8,9},{9,8},{10,11... | collective-permute-start | bytes 9437192 | tf_op jit(solution)/shard_map/ppermute | solution.py:81
  1.0 1.2 %copy-start.3 = (bf16[1,256,2048]{2,1,0:T(8,128)(2,1)S(1)}, bf16[1,256,2048]{2,1,0:T(8,128)(2,1)}, u32[]{:S(2)}) copy-start(bf16[1,256,2048]{2,1,0:T(8,128)(2,1)} %param.7) | copy-start | bytes 3145732
  2.4 10.9 %collective-permute-start.1 = (bf16[64,2048]{1,0:T(8,128)(2,1)S(1)}, bf16[64,2048]{1,0:T(8,128)(2,1)S(1)}, u32[]{:S(2)}, u32[]{:S(2)}) collective-permute-start(bf16[64,2048]{1,0:T(8,128)(2,1)S(1)} %get-tuple-element.34.refs_0_), channel_id=1, source_target_pairs={{0,4},{12,8},{1,5},{13,9},{2,6},{14,10},{3,7},{15,11},{16,20},{28,... | collective-permute-start | bytes 786440 | tf_op jit(solution)/shard_map/ppermute | solution.py:343
  6.8 0.7 copy-start.5
  7.5 0.7 copy-start.6
  8.2 3.7 %collective-permute-start.2 = (f32[4,256]{1,0:T(4,128)S(1)}, f32[4,256]{1,0:T(4,128)S(1)}, u32[]{:S(2)}, u32[]{:S(2)}) collective-permute-start(f32[4,256]{1,0:T(4,128)S(1)} %shard_map.74.refs_0_), channel_id=1, source_target_pairs={{0,2},{1,3},{2,0},{3,1},{4,6},{5,7},{6,4},{7,5},{8,10},{9,11},{10,... | collective-permute-start | bytes 12296 | tf_op jit(solution)/shard_map/ppermute | solution.py:81
  11.9 8.0 %collective-permute-start.4 = (bf16[64,2048]{1,0:T(8,128)(2,1)S(1)}, bf16[64,2048]{1,0:T(8,128)(2,1)S(1)}, u32[]{:S(2)}, u32[]{:S(2)}) collective-permute-start(bf16[64,2048]{1,0:T(8,128)(2,1)S(1)} %get-tuple-element.35.refs_0_), channel_id=1, source_target_pairs={{0,4},{12,8},{1,5},{13,9},{2,6},{14,10},{3,7},{15,11},{16,20},{28,... | collective-permute-start | bytes 786440 | tf_op jit(solution)/shard_map/ppermute | solution.py:343
  13.2 11.1 %collective-permute-start.7 = (bf16[64,2048]{1,0:T(8,128)(2,1)S(1)}, bf16[64,2048]{1,0:T(8,128)(2,1)S(1)}, u32[]{:S(2)}, u32[]{:S(2)}) collective-permute-start(bf16[64,2048]{1,0:T(8,128)(2,1)S(1)} %get-tuple-element.36.refs_0_), channel_id=1, source_target_pairs={{0,4},{12,8},{1,5},{13,9},{2,6},{14,10},{3,7},{15,11},{16,20},{28,... | collective-permute-start | bytes 786440 | tf_op jit(solution)/shard_map/ppermute | solution.py:343
  19.9 5.1 %collective-permute-start.3 = (bf16[64,2048]{1,0:T(8,128)(2,1)S(1)}, bf16[64,2048]{1,0:T(8,128)(2,1)S(1)}, u32[]{:S(2)}, u32[]{:S(2)}) collective-permute-start(bf16[64,2048]{1,0:T(8,128)(2,1)S(1)} %shard_map.76.refs_2_), channel_id=1, source_target_pairs={{4,8},{8,4},{5,9},{9,5},{6,10},{10,6},{7,11},{11,7},{20,24},{24,20... | collective-permute-start | bytes 786440 | tf_op jit(solution)/shard_map/ppermute | solution.py:351
  20.5 37.7 %copy-start.4 = (f32[1,2048]{1,0:T(1,128)S(1)}, f32[1,2048]{1,0:T(1,128)}, u32[]{:S(2)}) copy-start(f32[1,2048]{1,0:T(1,128)} %refs_2_.7) | copy-start | bytes 24580
  24.3 9.1 %collective-permute-start.6 = (bf16[64,2048]{1,0:T(8,128)(2,1)S(1)}, bf16[64,2048]{1,0:T(8,128)(2,1)S(1)}, u32[]{:S(2)}, u32[]{:S(2)}) collective-permute-start(bf16[64,2048]{1,0:T(8,128)(2,1)S(1)} %shard_map.77.refs_3_), channel_id=1, source_target_pairs={{4,8},{8,4},{5,9},{9,5},{6,10},{10,6},{7,11},{11,7},{20,24},{24,20... | collective-permute-start | bytes 786440 | tf_op jit(solution)/shard_map/ppermute | solution.py:351
  25.0 33.3 %copy-start.2 = (bf16[1,1,768,2048]{3,2,1,0:T(8,128)(2,1)S(1)}, bf16[1,1,768,2048]{3,2,1,0:T(8,128)(2,1)}, u32[]{:S(2)}) copy-start(bf16[1,1,768,2048]{3,2,1,0:T(8,128)(2,1)} %param.13) | copy-start | bytes 9437188
  25.0 12.1 %collective-permute-start = (bf16[64,2048]{1,0:T(8,128)(2,1)S(1)}, bf16[64,2048]{1,0:T(8,128)(2,1)S(1)}, u32[]{:S(2)}, u32[]{:S(2)}) collective-permute-start(bf16[64,2048]{1,0:T(8,128)(2,1)S(1)} %get-tuple-element.33.refs_0_), channel_id=1, source_target_pairs={{0,4},{12,8},{1,5},{13,9},{2,6},{14,10},{3,7},{15,11},{16,20},{28,... | collective-permute-start | bytes 786440 | tf_op jit(solution)/shard_map/ppermute | solution.py:343
  33.4 11.3 %collective-permute-start.5 = (bf16[64,2048]{1,0:T(8,128)(2,1)S(1)}, bf16[64,2048]{1,0:T(8,128)(2,1)S(1)}, u32[]{:S(2)}, u32[]{:S(2)}) collective-permute-start(bf16[64,2048]{1,0:T(8,128)(2,1)S(1)} %shard_map.78.refs_2_.refs_0_), channel_id=1, source_target_pairs={{4,0},{8,12},{5,1},{9,13},{6,2},{10,14},{7,3},{11,15},{20,16},{24,... | collective-permute-start | bytes 786440 | tf_op jit(solution)/shard_map/ppermute | solution.py:359
  34.7 23.5 %copy-start.1 = (bf16[1,1,2048,768]{3,2,1,0:T(8,128)(2,1)S(1)}, bf16[1,1,2048,768]{3,2,1,0:T(8,128)(2,1)}, u32[]{:S(2)}) copy-start(bf16[1,1,2048,768]{3,2,1,0:T(8,128)(2,1)} %param.12) | copy-start | bytes 9437188
  34.9 23.4 %copy-start = (bf16[1,1,2048,768]{3,2,1,0:T(8,128)(2,1)S(1)}, bf16[1,1,2048,768]{3,2,1,0:T(8,128)(2,1)}, u32[]{:S(2)}) copy-start(bf16[1,1,2048,768]{3,2,1,0:T(8,128)(2,1)} %param.11) | copy-start | bytes 9437188
  37.1 11.0 %collective-permute-start.9 = (bf16[64,2048]{1,0:T(8,128)(2,1)S(1)}, bf16[64,2048]{1,0:T(8,128)(2,1)S(1)}, u32[]{:S(2)}, u32[]{:S(2)}) collective-permute-start(bf16[64,2048]{1,0:T(8,128)(2,1)S(1)} %shard_map.80.refs_2_.refs_0_), channel_id=1, source_target_pairs={{4,0},{8,12},{5,1},{9,13},{6,2},{10,14},{7,3},{11,15},{20,16},{24,... | collective-permute-start | bytes 786440 | tf_op jit(solution)/shard_map/ppermute | solution.py:359
  44.6 4.1 %collective-permute-start.10 = (bf16[64,2048]{1,0:T(8,128)(2,1)S(1)}, bf16[64,2048]{1,0:T(8,128)(2,1)S(1)}, u32[]{:S(2)}, u32[]{:S(2)}) collective-permute-start(bf16[64,2048]{1,0:T(8,128)(2,1)S(1)} %shard_map.79.refs_3_), channel_id=1, source_target_pairs={{4,8},{8,4},{5,9},{9,5},{6,10},{10,6},{7,11},{11,7},{20,24},{24,20... | collective-permute-start | bytes 786440 | tf_op jit(solution)/shard_map/ppermute | solution.py:351
  48.1 2.3 %collective-permute-start.8 = (bf16[64,2048]{1,0:T(8,128)(2,1)S(1)}, bf16[64,2048]{1,0:T(8,128)(2,1)S(1)}, u32[]{:S(2)}, u32[]{:S(2)}) collective-permute-start(bf16[64,2048]{1,0:T(8,128)(2,1)S(1)} %shard_map.82.refs_3_), channel_id=1, source_target_pairs={{4,8},{8,4},{5,9},{9,5},{6,10},{10,6},{7,11},{11,7},{20,24},{24,20... | collective-permute-start | bytes 786440 | tf_op jit(solution)/shard_map/ppermute | solution.py:351
  48.8 6.4 %collective-permute-start.13 = (bf16[64,2048]{1,0:T(8,128)(2,1)S(1)}, bf16[64,2048]{1,0:T(8,128)(2,1)S(1)}, u32[]{:S(2)}, u32[]{:S(2)}) collective-permute-start(bf16[64,2048]{1,0:T(8,128)(2,1)S(1)} %shard_map.81.refs_2_.refs_0_), channel_id=1, source_target_pairs={{0,2},{1,3},{2,0},{3,1},{4,6},{5,7},{6,4},{7,5},{8,10},{9,11},{10,... | collective-permute-start | bytes 786440 | tf_op jit(solution)/shard_map/ppermute | solution.py:323
  50.4 16.8 %collective-permute-start.12 = (bf16[64,2048]{1,0:T(8,128)(2,1)S(1)}, bf16[64,2048]{1,0:T(8,128)(2,1)S(1)}, u32[]{:S(2)}, u32[]{:S(2)}) collective-permute-start(bf16[64,2048]{1,0:T(8,128)(2,1)S(1)} %shard_map.83.refs_2_.refs_0_), channel_id=1, source_target_pairs={{4,0},{8,12},{5,1},{9,13},{6,2},{10,14},{7,3},{11,15},{20,16},{24,... | collective-permute-start | bytes 786440 | tf_op jit(solution)/shard_map/ppermute | solution.py:359
  55.2 16.7 %collective-permute-start.11 = (bf16[64,2048]{1,0:T(8,128)(2,1)S(1)}, bf16[64,2048]{1,0:T(8,128)(2,1)S(1)}, u32[]{:S(2)}, u32[]{:S(2)}) collective-permute-start(bf16[64,2048]{1,0:T(8,128)(2,1)S(1)} %shard_map.85.refs_10_.refs_0_), channel_id=1, source_target_pairs={{4,0},{8,12},{5,1},{9,13},{6,2},{10,14},{7,3},{11,15},{20,16},{24,... | collective-permute-start | bytes 786440 | tf_op jit(solution)/shard_map/ppermute | solution.py:359
  56.7 16.8 %collective-permute-start.20 = (bf16[64,2048]{1,0:T(8,128)(2,1)S(1)}, bf16[64,2048]{1,0:T(8,128)(2,1)S(1)}, u32[]{:S(2)}, u32[]{:S(2)}) collective-permute-start(bf16[64,2048]{1,0:T(8,128)(2,1)S(1)} %shard_map.84.refs_3_.refs_0_.refs_2_), channel_id=1, source_target_pairs={{0,2},{1,3},{2,0},{3,1},{4,6},{5,7},{6,4},{7,5},{8,10},{9,11},{10,... | collective-permute-start | bytes 786440 | tf_op jit(solution)/shard_map/ppermute | solution.py:323
  61.2 15.3 %collective-permute-start.19 = (bf16[128,1024]{1,0:T(8,128)(2,1)S(1)}, bf16[128,1024]{1,0:T(8,128)(2,1)S(1)}, u32[]{:S(2)}, u32[]{:S(2)}) collective-permute-start(bf16[128,1024]{1,0:T(8,128)(2,1)S(1)} %get-tuple-element.37.refs_2_), channel_id=1, source_target_pairs={{0,4},{4,0},{8,12},{12,8},{1,5},{5,1},{9,13},{13,9},{2,6},{6,2},{1... | collective-permute-start | bytes 786440 | tf_op jit(solution)/shard_map/ppermute | solution.py:323
  67.3 9.3 %collective-permute-start.18 = (bf16[64,2048]{1,0:T(8,128)(2,1)S(1)}, bf16[64,2048]{1,0:T(8,128)(2,1)S(1)}, u32[]{:S(2)}, u32[]{:S(2)}) collective-permute-start(bf16[64,2048]{1,0:T(8,128)(2,1)S(1)} %shard_map.87.refs_2_.refs_0_), channel_id=1, source_target_pairs={{0,2},{1,3},{2,0},{3,1},{4,6},{5,7},{6,4},{7,5},{8,10},{9,11},{10,... | collective-permute-start | bytes 786440 | tf_op jit(solution)/shard_map/ppermute | solution.py:323
  72.0 9.9 %collective-permute-start.17 = (bf16[64,2048]{1,0:T(8,128)(2,1)S(1)}, bf16[64,2048]{1,0:T(8,128)(2,1)S(1)}, u32[]{:S(2)}, u32[]{:S(2)}) collective-permute-start(bf16[64,2048]{1,0:T(8,128)(2,1)S(1)} %shard_map.88.refs_10_.refs_0_.refs_2_), channel_id=1, source_target_pairs={{0,2},{1,3},{2,0},{3,1},{4,6},{5,7},{6,4},{7,5},{8,10},{9,11},{10,... | collective-permute-start | bytes 786440 | tf_op jit(solution)/shard_map/ppermute | solution.py:323
  76.4 11.2 %collective-permute-start.24 = (bf16[128,1024]{1,0:T(8,128)(2,1)S(1)}, bf16[128,1024]{1,0:T(8,128)(2,1)S(1)}, u32[]{:S(2)}, u32[]{:S(2)}) collective-permute-start(bf16[128,1024]{1,0:T(8,128)(2,1)S(1)} %get-tuple-element.39.refs_2_), channel_id=1, source_target_pairs={{0,4},{4,0},{8,12},{12,8},{1,5},{5,1},{9,13},{13,9},{2,6},{6,2},{1... | collective-permute-start | bytes 786440 | tf_op jit(solution)/shard_map/ppermute | solution.py:323
  79.5 12.0 %collective-permute-start.22 = (bf16[64,2048]{1,0:T(8,128)(2,1)S(1)}, bf16[64,2048]{1,0:T(8,128)(2,1)S(1)}, u32[]{:S(2)}, u32[]{:S(2)}) collective-permute-start(bf16[64,2048]{1,0:T(8,128)(2,1)S(1)} %get-tuple-element.41.refs_10_), channel_id=1, source_target_pairs={{0,2},{1,3},{2,0},{3,1},{4,6},{5,7},{6,4},{7,5},{8,10},{9,11},{10,... | collective-permute-start | bytes 786440 | tf_op jit(solution)/shard_map/ppermute | solution.py:323
  84.8 9.3 %collective-permute-start.21 = (bf16[64,2048]{1,0:T(8,128)(2,1)S(1)}, bf16[64,2048]{1,0:T(8,128)(2,1)S(1)}, u32[]{:S(2)}, u32[]{:S(2)}) collective-permute-start(bf16[64,2048]{1,0:T(8,128)(2,1)S(1)} %get-tuple-element.43.refs_2_), channel_id=1, source_target_pairs={{0,2},{1,3},{2,0},{3,1},{4,6},{5,7},{6,4},{7,5},{8,10},{9,11},{10,... | collective-permute-start | bytes 786440 | tf_op jit(solution)/shard_map/ppermute | solution.py:323
  84.8 6.6 %collective-permute-start.23 = (bf16[128,512]{1,0:T(8,128)(2,1)S(1)}, bf16[128,512]{1,0:T(8,128)(2,1)S(1)}, u32[]{:S(2)}, u32[]{:S(2)}) collective-permute-start(bf16[128,512]{1,0:T(8,128)(2,1)S(1)} %get-tuple-element.40.refs_10_), channel_id=1, source_target_pairs={{0,8},{4,12},{8,0},{12,4},{1,9},{5,13},{9,1},{13,5},{2,10},{6,14},... | collective-permute-start | bytes 393224 | tf_op jit(solution)/shard_map/ppermute | solution.py:323
  87.7 8.6 %collective-permute-start.28 = (bf16[128,512]{1,0:T(8,128)(2,1)S(1)}, bf16[128,512]{1,0:T(8,128)(2,1)S(1)}, u32[]{:S(2)}, u32[]{:S(2)}) collective-permute-start(bf16[128,512]{1,0:T(8,128)(2,1)S(1)} %get-tuple-element.47.refs_2_), channel_id=1, source_target_pairs={{0,8},{4,12},{8,0},{12,4},{1,9},{5,13},{9,1},{13,5},{2,10},{6,14},... | collective-permute-start | bytes 393224 | tf_op jit(solution)/shard_map/ppermute | solution.py:323
  91.6 6.1 %collective-permute-start.27 = (bf16[64,1024]{1,0:T(8,128)(2,1)S(1)}, bf16[64,1024]{1,0:T(8,128)(2,1)S(1)}, u32[]{:S(2)}, u32[]{:S(2)}) collective-permute-start(bf16[64,1024]{1,0:T(8,128)(2,1)S(1)} %get-tuple-element.49.refs_2_), channel_id=1, source_target_pairs={{0,4},{4,0},{8,12},{12,8},{1,5},{5,1},{9,13},{13,9},{2,6},{6,2},{1... | collective-permute-start | bytes 393224 | tf_op jit(solution)/shard_map/ppermute | solution.py:323
  94.1 6.2 %collective-permute-start.25 = (bf16[64,1024]{1,0:T(8,128)(2,1)S(1)}, bf16[64,1024]{1,0:T(8,128)(2,1)S(1)}, u32[]{:S(2)}, u32[]{:S(2)}) collective-permute-start(bf16[64,1024]{1,0:T(8,128)(2,1)S(1)} %get-tuple-element.51.refs_2_), channel_id=1, source_target_pairs={{0,4},{4,0},{8,12},{12,8},{1,5},{5,1},{9,13},{13,9},{2,6},{6,2},{1... | collective-permute-start | bytes 393224 | tf_op jit(solution)/shard_map/ppermute | solution.py:323
  94.2 6.0 %collective-permute-start.26 = (bf16[64,512]{1,0:T(8,128)(2,1)S(1)}, bf16[64,512]{1,0:T(8,128)(2,1)S(1)}, u32[]{:S(2)}, u32[]{:S(2)}) collective-permute-start(bf16[64,512]{1,0:T(8,128)(2,1)S(1)} %get-tuple-element.48.refs_2_), channel_id=1, source_target_pairs={{0,2},{1,3},{2,0},{3,1},{4,6},{5,7},{6,4},{7,5},{8,10},{9,11},{10,... | collective-permute-start | bytes 196616 | tf_op jit(solution)/shard_map/ppermute | solution.py:323
  96.3 5.9 %collective-permute-start.30 = (bf16[64,512]{1,0:T(8,128)(2,1)S(1)}, bf16[64,512]{1,0:T(8,128)(2,1)S(1)}, u32[]{:S(2)}, u32[]{:S(2)}) collective-permute-start(bf16[64,512]{1,0:T(8,128)(2,1)S(1)} %get-tuple-element.55.refs_2_), channel_id=1, source_target_pairs={{0,2},{1,3},{2,0},{3,1},{4,6},{5,7},{6,4},{7,5},{8,10},{9,11},{10,... | collective-permute-start | bytes 196616 | tf_op jit(solution)/shard_map/ppermute | solution.py:323
  97.7 5.2 %collective-permute-start.31 = (bf16[64,512]{1,0:T(8,128)(2,1)S(1)}, bf16[64,512]{1,0:T(8,128)(2,1)S(1)}, u32[]{:S(2)}, u32[]{:S(2)}) collective-permute-start(bf16[64,512]{1,0:T(8,128)(2,1)S(1)} %get-tuple-element.56.refs_3_), channel_id=1, source_target_pairs={{0,8},{4,12},{8,0},{12,4},{1,9},{5,13},{9,1},{13,5},{2,10},{6,14},... | collective-permute-start | bytes 196616 | tf_op jit(solution)/shard_map/ppermute | solution.py:323
  100.3 5.9 %collective-permute-start.29 = (bf16[64,512]{1,0:T(8,128)(2,1)S(1)}, bf16[64,512]{1,0:T(8,128)(2,1)S(1)}, u32[]{:S(2)}, u32[]{:S(2)}) collective-permute-start(bf16[64,512]{1,0:T(8,128)(2,1)S(1)} %get-tuple-element.58.refs_3_), channel_id=1, source_target_pairs={{0,8},{4,12},{8,0},{12,4},{1,9},{5,13},{9,1},{13,5},{2,10},{6,14},... | collective-permute-start | bytes 196616 | tf_op jit(solution)/shard_map/ppermute | solution.py:323
